TPU v7x, 1024 devices: a whole 4x8x16 slice. The times are simulated.
1024 devices in a mesh: section: 16 (over z), expert: 64 (over x, y, core).
Axes of the slice: x: 4, y: 8, z: 16, core: 2. Of those that a mesh axis runs over, the one named last changes fastest.
Arguments:
- out_grad: bfloat16 [16, 2048, 2048], P('section', 'expert'), may hold values from -6 to 6
- layer_input: bfloat16 [16, 2048, 2048], P('section', 'expert'), may hold values from -6 to 6
- router_weight: bfloat16 [16, 2048, 64], P('section'), may hold values from -0.125 to 0.125
- expert_ids: int32 [16, 2048, 8], P('section', 'expert'), may hold values from 0 to 63, all different within a row; in each aligned block of 32 rows (0 to 31, 32 to 63, ..., all dimensions but the last counted through in order) at most 6 rows name the same one
- hidden_act: bfloat16 [16, 64, 384, 384], P('section', 'expert'), may hold values from -6 to 6
- down_weight: bfloat16 [16, 64, 384, 2048], P('section', 'expert'), may hold values from -0.3125 to 0.3125
Outputs:
- sent_grad: bfloat16 [16, 2048, 2048], P('section', 'expert')
- hidden_grad: bfloat16 [16, 64, 384, 384], P('section', 'expert')
- router_grad: float32 [16, 2048, 64], P('section', 'expert')
Inputs may be any that keep to these rules, and one draw needn't show every extreme that they name: `expert_ids`: each token names 8 different experts. In each aligned block of 32 tokens (the tokens of one device) no expert is named by more than 6 tokens, a bound that some block reaches.
All inputs are finite; a program needn't handle non-finite values.
Results may differ from a plain program's by a relative error of at most 0.0095.
Values may be sent and summed in bfloat16 or wider, within the bound.
No kernel may reach another device: no remote copies, remote signals or barrier semaphores. Data moves between devices by JAX's collectives and lax.ppermute only.
A program may use at most 32 MiB of HBM per device.

v0:
```python
import jax
import jax.numpy as jnp
from jax import lax
from jax.sharding import PartitionSpec as P


def shifted(shard, axis, by):
    count = lax.axis_size(axis)
    return lax.ppermute(shard, axis, [(i, (i + by) % count) for i in range(count)])


def shards(out_grad, layer_input, router_weight, expert_ids, hidden_act, down_weight):
    out_grads = out_grad[0]
    inputs = layer_input[0]
    router = router_weight[0]
    chosen_ids = expert_ids[0]
    hidden = hidden_act[0, 0]
    w_down = down_weight[0, 0]
    peer_count = lax.axis_size("expert")
    tokens_here = chosen_ids.shape[0]
    choices_per = chosen_ids.shape[1]
    experts = router.shape[1]
    capacity = hidden.shape[0] // peer_count
    logits = jnp.dot(inputs, router, preferred_element_type=jnp.float32)
    picked = (chosen_ids[:, :, None] == jnp.arange(experts, dtype=jnp.int32)[None, None, :]).astype(
        jnp.float32
    )
    chosen_logits = jnp.sum(picked * logits[:, None, :], axis=-1)
    weights = jnp.exp(chosen_logits)
    gate_vals = (weights / jnp.sum(weights, axis=-1, keepdims=True)).astype(jnp.bfloat16)
    flat_hot = picked.reshape(tokens_here * choices_per, experts)
    before = jnp.cumsum(flat_hot, axis=0) - flat_hot
    slot_rank = (
        jnp.sum(before * flat_hot, axis=-1).astype(jnp.int32).reshape(tokens_here, choices_per)
    )
    position = chosen_ids * capacity + slot_rank
    placing = (
        position[:, :, None] == jnp.arange(experts * capacity, dtype=jnp.int32)[None, None, :]
    ).astype(jnp.bfloat16)
    send_grads = jnp.einsum(
        "tks,td->sd", placing, out_grads, preferred_element_type=jnp.float32
    ).astype(jnp.bfloat16)
    send_gates = jnp.einsum(
        "tks,tk->s", placing, gate_vals, preferred_element_type=jnp.float32
    ).astype(jnp.bfloat16)
    send_grads = send_grads.reshape(experts, capacity, send_grads.shape[-1])
    send_gates = send_gates.reshape(experts, capacity)
    recv_grads, recv_gates = (
        lax.all_to_all(send_grads, "expert", split_axis=0, concat_axis=0, tiled=True),
        lax.all_to_all(send_gates, "expert", split_axis=0, concat_axis=0, tiled=True),
    )
    slot_rows = recv_grads.reshape(-1, recv_grads.shape[-1])
    expert_out = jnp.dot(hidden, w_down, preferred_element_type=jnp.float32)
    slot_dg = jnp.sum(slot_rows.astype(jnp.float32) * expert_out, axis=-1)
    scaled = (
        recv_gates.reshape(-1).astype(jnp.float32)[:, None] * slot_rows.astype(jnp.float32)
    ).astype(jnp.bfloat16)
    hidden_grad = lax.dot_general(
        scaled, w_down, (((1,), (1,)), ((), ())), preferred_element_type=jnp.float32
    ).astype(jnp.bfloat16)
    returned = lax.all_to_all(
        slot_dg.reshape(peer_count, capacity), "expert", split_axis=0, concat_axis=0, tiled=True
    )
    gate_grad = jnp.take(returned.reshape(-1), position, axis=0)
    gate_float = gate_vals.astype(jnp.float32)
    dchosen = gate_float * (gate_grad - jnp.sum(gate_float * gate_grad, axis=-1, keepdims=True))
    logit_grad = jnp.sum(dchosen[:, :, None] * picked, axis=1).astype(jnp.bfloat16)
    router_part = lax.dot_general(
        logit_grad, router, (((1,), (1,)), ((), ())), preferred_element_type=jnp.float32
    )
    input_grad = (out_grads.astype(jnp.float32) + router_part).astype(jnp.bfloat16)
    to_previous = shifted(input_grad[None], "section", -1)
    router_grad = lax.psum_scatter(
        jnp.einsum("td,te->de", inputs, logit_grad, preferred_element_type=jnp.float32),
        "expert",
        scatter_dimension=0,
        tiled=True,
    )
    return (to_previous, hidden_grad[None, None], router_grad[None])


def solution(mesh):
    placed = (
        P("section", "expert", None),
        P("section", "expert", None),
        P("section", None, None),
        P("section", "expert", None),
        P("section", "expert", None, None),
        P("section", "expert", None, None),
    )
    return jax.shard_map(
        shards,
        mesh=mesh,
        in_specs=placed,
        out_specs=(
            P("section", "expert", None),
            P("section", "expert", None, None),
            P("section", "expert", None),
        ),
        check_vma=False,
    )
```

profile of v0, /device:TPU:1, one launch (start us, length us, event | category | flops | bytes accessed | tf_op | source)
XLA Modules:
  0.0 289.6 jit_solution(3926853452517745039)
XLA Ops:
  7.2 0.0 copy-start
  7.2 0.9 copy.27
  8.1 0.1 eq.55
  8.1 0.1 eq.51
  8.3 0.6 reduce-window.6
  8.9 0.2 slice_reduce_fusion
  9.1 0.1 fusion.22
  9.2 0.1 convert_element_type.103
  9.3 0.2 convert_reduce_fusion
  9.5 1.5 convolution_convert_fusion
  11.0 1.6 reshape.161
  12.6 0.0 copy-start.1
  12.6 0.0 copy-start.2
  12.6 19.2 %all-to-all-start = ((bf16[64,6,2048]{2,1,0:T(8,128)(2,1)}), bf16[64,6,2048]{2,1,0:T(8,128)(2,1)}, u32[]{:S(2)}, u32[]{:S(2)}) async-start(bf16[64,6,2048]{2,1,0:T(8,128)(2,1)} %reshape.161), calls=%async_computation | async-start | bytes 4194304 | tf_op jit(solution)/shard_map/all_to_all | solution.py:49
  31.8 0.1 convert_element_type.109
  31.9 0.1 reshape.167
  32.0 0.0 copy-done.1
  32.0 0.0 copy-done.2
  32.1 0.2 fusion.14
  32.2 0.2 select_reduce_fusion.1
  32.4 0.1 exponential_reduce_fusion
  32.6 0.0 copy-start.4
  32.6 50.5 %all-to-all-done = bf16[64,6,2048]{2,1,0:T(8,128)(2,1)} async-done(((bf16[64,6,2048]{2,1,0:T(8,128)(2,1)}), bf16[64,6,2048]{2,1,0:T(8,128)(2,1)}, u32[]{:S(2)}, u32[]{:S(2)}) %all-to-all-start) | async-done | bytes 1572896 | tf_op jit(solution)/shard_map/all_to_all | solution.py:49
  83.1 4.0 %reshape.163 = f32[384,2048]{1,0:T(8,128)} reshape(bf16[64,6,2048]{2,1,0:T(8,128)(2,1)} %all-to-all-done) | data formatting | bytes 4718592 | tf_op jit(solution)/shard_map/convert_element_type | solution.py:54
  87.1 0.0 copy-done
  87.1 0.0 copy-done.4
  87.1 3.0 %multiply_reduce_fusion = f32[384]{0:T(512)S(1)} fusion(f32[384,2048]{1,0:T(8,128)} %reshape.163, bf16[1,1,384,2048]{3,2,1,0:T(8,128)(2,1)S(1)} %copy-done, bf16[1,1,384,384]{3,2,1,0:T(8,128)(2,1)S(1)} %copy-done.4), kind=kOutput, calls=%fused_computation.2 | convolution fusion | flops 605552256 | bytes 5015040 | tf_op jit(solution)/shard_map/dot_general | solution.py:53
  90.1 0.8 all_to_all.16
  90.8 5.8 %all-to-all-start.1 = ((f32[64,1,6]{2,1,0:T(1,128)}), f32[64,1,6]{2,1,0:T(1,128)S(1)}, u32[]{:S(2)}, u32[]{:S(2)}) async-start(f32[64,1,6]{2,1,0:T(1,128)} %bitcast.7), calls=%async_computation.1 | async-start | bytes 65536 | tf_op jit(solution)/shard_map/all_to_all | solution.py:61
  96.7 9.2 %all-to-all-done.1 = f32[64,1,6]{2,1,0:T(1,128)S(1)} async-done(((f32[64,1,6]{2,1,0:T(1,128)}), f32[64,1,6]{2,1,0:T(1,128)S(1)}, u32[]{:S(2)}, u32[]{:S(2)}) %all-to-all-start.1) | async-done | bytes 1568 | tf_op jit(solution)/shard_map/all_to_all | solution.py:61
  105.9 0.5 broadcast.118
  106.4 0.7 reduce.7
  107.1 0.1 reshape.162
  107.3 0.0 copy-start.3
  107.3 1.9 gather_fusion
  109.2 0.1 reshape.166
  109.3 0.2 fusion.24
  109.5 0.3 convolution_reduce_fusion
  109.8 0.8 all_to_all.20
  110.6 4.7 %all-to-all-start.2 = ((bf16[64,1,6]{2,1,0:T(2,128)(2,1)}), bf16[64,1,6]{2,1,0:T(2,128)(2,1)S(1)}, u32[]{:S(2)}, u32[]{:S(2)}) async-start(bf16[64,1,6]{2,1,0:T(2,128)(2,1)} %all_to_all.20), calls=%async_computation.2 | async-start | bytes 65536 | tf_op jit(solution)/shard_map/all_to_all | solution.py:50
  115.3 0.0 reduce-scatter.4.cloned.1.call-start
  115.3 0.1 convert_multiply_fusion
  115.4 0.2 select_reduce_fusion
  115.5 0.3 convolution_bitcast_fusion
  115.8 0.0 copy-done.3
  115.8 0.2 fusion.1
  116.0 1.3 copy.36
  117.3 0.0 reduce-scatter.4.cloned.1.call-update
  117.3 10.6 %collective-permute-start = (bf16[1,32,2048]{2,1,0:T(8,128)(2,1)S(1)}, bf16[1,32,2048]{2,1,0:T(8,128)(2,1)S(1)}, u32[]{:S(2)}, u32[]{:S(2)}) collective-permute-start(bf16[1,32,2048]{2,1,0:T(8,128)(2,1)S(1)} %fusion.1), channel_id=1, source_target_pairs={{0,960},{64,0},{128,64},{192,128},{256,192},{320,256},{384,320},{4... | collective-permute-start | bytes 393224 | tf_op jit(solution)/shard_map/ppermute | solution.py:9
  127.9 0.0 all-to-all-done.2
  128.0 3.4 %multiply_convert_fusion = bf16[64,6,2048]{2,1,0:T(8,128)(2,1)} fusion(f32[64,6]{1,0:T(8,128)S(1)} %bitcast.70, bf16[64,6,2048]{2,1,0:T(8,128)(2,1)} %all-to-all-done), kind=kLoop, calls=%fused_computation.1 | loop fusion | flops 2359296 | bytes 3147264 | tf_op jit(solution)/shard_map/convert_element_type | solution.py:57
  131.3 2.6 convert_element_type.117
  133.9 1.7 fusion.8
  135.6 0.0 collective-permute-done
  135.6 144.9 %reduce-scatter.4.cloned.1.call-done = f32[32,64]{1,0:T(8,128)} async-done(((f32[2048,64]{1,0:T(8,128)}), f32[32,64]{1,0:T(8,128)}) %reduce-scatter.4.cloned.1.call-update) | async-done | bytes 8208
  280.6 0.8 copy.37
  281.4 0.7 copy.34
  282.1 0.7 copy.43
  (8 shorter events, 0.1 us)
Async XLA Ops:
  7.2 80.0 %copy-start = (bf16[1,1,384,2048]{3,2,1,0:T(8,128)(2,1)S(1)}, bf16[1,1,384,2048]{3,2,1,0:T(8,128)(2,1)}, u32[]{:S(2)}) copy-start(bf16[1,1,384,2048]{3,2,1,0:T(8,128)(2,1)} %param.11) | copy-start | bytes 4718596
  12.6 19.4 %copy-start.1 = (bf16[1,2048,64]{1,2,0:T(8,128)(2,1)S(1)}, bf16[1,2048,64]{1,2,0:T(8,128)(2,1)}, u32[]{:S(2)}) copy-start(bf16[1,2048,64]{1,2,0:T(8,128)(2,1)} %param.8) | copy-start | bytes 786436
  12.6 19.4 %copy-start.2 = (bf16[1,32,2048]{2,1,0:T(8,128)(2,1)S(1)}, bf16[1,32,2048]{2,1,0:T(8,128)(2,1)}, u32[]{:S(2)}) copy-start(bf16[1,32,2048]{2,1,0:T(8,128)(2,1)} %param.7) | copy-start | bytes 393220
  12.6 70.5 %all-to-all-start = ((bf16[64,6,2048]{2,1,0:T(8,128)(2,1)}), bf16[64,6,2048]{2,1,0:T(8,128)(2,1)}, u32[]{:S(2)}, u32[]{:S(2)}) async-start(bf16[64,6,2048]{2,1,0:T(8,128)(2,1)} %reshape.161), calls=%async_computation | async-start | bytes 4194304 | tf_op jit(solution)/shard_map/all_to_all | solution.py:49
  32.6 54.6 %copy-start.4 = (bf16[1,1,384,384]{3,2,1,0:T(8,128)(2,1)S(1)}, bf16[1,1,384,384]{3,2,1,0:T(8,128)(2,1)}, u32[]{:S(2)}) copy-start(bf16[1,1,384,384]{3,2,1,0:T(8,128)(2,1)} %param.10) | copy-start | bytes 884740
  90.8 15.0 %all-to-all-start.1 = ((f32[64,1,6]{2,1,0:T(1,128)}), f32[64,1,6]{2,1,0:T(1,128)S(1)}, u32[]{:S(2)}, u32[]{:S(2)}) async-start(f32[64,1,6]{2,1,0:T(1,128)} %bitcast.7), calls=%async_computation.1 | async-start | bytes 65536 | tf_op jit(solution)/shard_map/all_to_all | solution.py:61
  107.3 8.5 %copy-start.3 = (bf16[1,32,2048]{2,1,0:T(8,128)(2,1)S(1)}, bf16[1,32,2048]{2,1,0:T(8,128)(2,1)}, u32[]{:S(2)}) copy-start(bf16[1,32,2048]{2,1,0:T(8,128)(2,1)} %param.6) | copy-start | bytes 393220
  110.6 17.3 %all-to-all-start.2 = ((bf16[64,1,6]{2,1,0:T(2,128)(2,1)}), bf16[64,1,6]{2,1,0:T(2,128)(2,1)S(1)}, u32[]{:S(2)}, u32[]{:S(2)}) async-start(bf16[64,1,6]{2,1,0:T(2,128)(2,1)} %all_to_all.20), calls=%async_computation.2 | async-start | bytes 65536 | tf_op jit(solution)/shard_map/all_to_all | solution.py:50
  115.3 165.3 %reduce-scatter.4.cloned.1.call-start = ((), (), s32[]{:S(2)}) async-start(), calls=%async_computation.4 | async-start | bytes 1064960
  117.3 18.3 %collective-permute-start = (bf16[1,32,2048]{2,1,0:T(8,128)(2,1)S(1)}, bf16[1,32,2048]{2,1,0:T(8,128)(2,1)S(1)}, u32[]{:S(2)}, u32[]{:S(2)}) collective-permute-start(bf16[1,32,2048]{2,1,0:T(8,128)(2,1)S(1)} %fusion.1), channel_id=1, source_target_pairs={{0,960},{64,0},{128,64},{192,128},{256,192},{320,256},{384,320},{4... | collective-permute-start | bytes 393224 | tf_op jit(solution)/shard_map/ppermute | solution.py:9
Sparse Core Ops, SparseCore 0:
  121.8 158.7 reduce-scatter.3
where the time goes:
time: 294 us; the launch traced here: 290 us
  waiting for transfers between devices  205 us (70%)
  starting transfers between devices  40.3 us (14%)
  local copies, waits for them, and re-layouts  17.4 us (6%)
  between operations  14.2 us (5%)
  matrix products  7.04 us (2%)
  other arithmetic  5.85 us (2%)
    unnamed x2, waiting for transfers between devices  145 us
    all_to_all x1, waiting for transfers between devices, shards(): lax.all_to_all(send_grads, 'expert', split_axis=0, concat_axis=0, tiled=T...  50.5 us
    all_to_all x1, starting transfers between devices, shards(): lax.all_to_all(send_grads, 'expert', split_axis=0, concat_axis=0, tiled=T...  19.2 us
    ppermute x1, starting transfers between devices, shifted(): lax.ppermute(shard, axis, [(i, (i + by) % count) for i in range(count)])  10.6 us
    all_to_all x1, waiting for transfers between devices, shards(): lax.all_to_all(slot_dg.reshape(peer_count, capacity), 'expert', split_axi...  9.2 us
  transfers between devices with their start and end apart: 5, of which 3 were waited for; matrix products, arithmetic and copies ran while one was open for 4% of the time, Pallas kernels for 0%

commit v1 on v0

v1 whole, which is shorter than its diff:
```python
import jax
import jax.numpy as jnp
import numpy as np
from jax import lax
from jax.experimental import pallas as pl
from jax.experimental.pallas import tpu as pltpu
from jax.sharding import PartitionSpec as P

F32 = jnp.float32
BF16 = jnp.bfloat16
PEERS = 64
CAP = 6
TOK = 32
WIDE = 256
PARTS = 8
ROWS = PARTS * CAP
CHUNK = ROWS + 8
SLOTS = PEERS * CAP
GROUPS = 16


def dot(a, b, ca, cb):
    return lax.dot_general(a, b, (((ca,), (cb,)), ((), ())), preferred_element_type=F32)


def iota(shape, dim):
    return lax.broadcasted_iota(jnp.int32, shape, dim)


def compaction():
    p = np.zeros((8 * ROWS, 8 * ROWS), np.float32)
    for part in range(PARTS):
        for b in range(8):
            for c in range(CAP):
                p[part * ROWS + b * CAP + c, b * ROWS + part * CAP + c] = 1
    return p


def spreading():
    m = np.zeros((128, CAP * 128), np.float32)
    for piece in range(3):
        for b in range(4):
            for c in range(CAP):
                row = piece * 32 + b * CAP + c
                m[row, c * 128 + b * TOK : c * 128 + (b + 1) * TOK] = 1
    return m


def pack_kernel(og_ref, li_ref, rw_ref, ids_ref, send_ref, gate_ref, code_ref, gt_ref, ct_ref):
    ids = ids_ref[...]
    logits = dot(rw_ref[...], li_ref[...], 1, 1)
    expert = iota((PEERS, TOK), 0)
    named = jnp.zeros((PEERS, TOK), F32)
    for k in range(8):
        named = jnp.where(ids[k : k + 1, :] == expert, 1.0, named)
    weights = jnp.where(named > 0.5, jnp.exp(logits), 0.0)
    gates = (weights / jnp.sum(weights, axis=0, keepdims=True)).astype(BF16)
    token = iota((TOK, WIDE), 0)
    lane = iota((TOK, WIDE), 1) & (TOK - 1)
    tile = jnp.where(token == lane, 1.0, 0.0).astype(BF16)
    ahead = jnp.where(token < lane, 1.0, 0.0).astype(BF16)
    named_b = named.astype(BF16)
    code = jnp.where(dot(named_b, tile, 1, 0) > 0.5, dot(named_b, ahead, 1, 0), -1.0)
    ct_ref[...] = code
    gt_ref[...] = dot(gates, tile, 1, 0)
    gates_f = gates.astype(F32)
    gate_ref[...] = gates_f
    code_ref[...] = code[:, :TOK]

    choice = iota((8, TOK), 0)
    compact = jnp.zeros((8, TOK), F32)
    for k in range(8):
        one = jnp.sum(jnp.where(ids[k : k + 1, :] == expert, gates_f, 0.0), axis=0, keepdims=True)
        compact = jnp.where(choice == k, one, compact)
    t128, l128 = iota((TOK, 128), 0), iota((TOK, 128), 1)
    put_ids = jnp.where(t128 == l128, 1.0, 0.0).astype(BF16)
    put_gates = jnp.where(t128 + TOK == l128, 1.0, 0.0).astype(BF16)
    info = dot(ids.astype(F32).astype(BF16), put_ids, 1, 0) + dot(
        compact.astype(BF16), put_gates, 1, 0
    )
    send_ref[:, ROWS:, 128:] = jnp.broadcast_to(info.astype(BF16)[None], (PEERS, 8, 128))

    spread = dot(li_ref[...], tile[:, :128], 0, 0).reshape(PEERS, 4, 8, 128)
    quarter = iota((PEERS, 8, 128), 2) // TOK
    columns = spread[:, 0]
    for h in range(1, 4):
        columns = jnp.where(quarter == h, spread[:, h], columns)
    send_ref[:, ROWS:, :128] = columns.astype(BF16)

    stacked = jnp.concatenate(
        [og_ref[:, j * WIDE : (j + 1) * WIDE] for j in range(PARTS)], axis=0
    )
    row = iota((ROWS, WIDE), 0)
    part = jnp.zeros((ROWS, WIDE), jnp.int32)
    for j in range(1, PARTS):
        part = part + jnp.where(row >= j * CAP, 1, 0)
    slot = jnp.where(iota((ROWS, WIDE), 1) // TOK == part, row - part * CAP, -2).astype(F32)

    def step(i, carry):
        picks = []
        for u in range(8):
            at = pl.ds(i * 8 + u, 1)
            hit = jnp.broadcast_to(ct_ref[at, :], (ROWS, WIDE)) == slot
            picks.append(
                jnp.where(hit, jnp.broadcast_to(gt_ref[at, :], (ROWS, WIDE)), 0.0).astype(BF16)
            )
        rows = dot(jnp.concatenate(picks, axis=0), stacked, 1, 0).astype(BF16)
        send_ref[pl.ds(i * 8, 8), :ROWS, :] = rows.reshape(8, ROWS, WIDE)
        return carry

    lax.fori_loop(0, PEERS // 8, step, 0)


def expert_kernel(recv_ref, w_ref, h_ref, perm_ref, hg_ref, sdg_ref, rows_ref):
    perm = perm_ref[...]
    for g in range(8):
        chunk = recv_ref[g * 8 : (g + 1) * 8, :, :].reshape(8 * ROWS, WIDE)
        moved = dot(perm, chunk, 1, 0).astype(BF16)
        for j in range(PARTS):
            rows_ref[g * ROWS : (g + 1) * ROWS, j * WIDE : (j + 1) * WIDE] = moved[
                j * ROWS : (j + 1) * ROWS
            ]
    grad = dot(rows_ref[...], w_ref[...], 1, 1)
    hg_ref[...] = grad.astype(BF16)
    prod = grad * h_ref[...].astype(F32)
    part = prod[:, :128] + prod[:, 128:256] + prod[:, 256:]
    gap = jnp.zeros((8, 128), F32)
    pieces = []
    for g in range(GROUPS):
        pieces += [part[g * 24 : (g + 1) * 24], gap]
    padded = jnp.concatenate(pieces, axis=0)
    line = jnp.sum(padded.T, axis=0, keepdims=True)
    which = iota((8, 128), 0) & 3
    out = jnp.zeros((8, 128), F32)
    for t in range(4):
        out = jnp.where(which == t, line[:, t * 128 : (t + 1) * 128], out)
    sdg_ref[...] = jnp.broadcast_to(out[None], (PEERS // 2, 8, 128)).reshape(PEERS * 4, 128)


def side_kernel(ext_ref, sdg_ref, gate_ref, code_ref, cols_ref, ready_ref):
    ready_ref[...] = sdg_ref[...]
    expert = iota((PEERS, 128), 0).astype(F32)
    row, col = iota((128, 128), 0), iota((128, 128), 1)
    ahead = jnp.where((row // TOK == col // TOK) & (row < col), 1.0, 0.0).astype(BF16)
    quarter = iota((8, 128), 1) // TOK

    def gather(blocks, at):
        out = None
        for i, block in enumerate(blocks):
            shift = (i - at) * TOK % 128
            moved = pltpu.roll(block, shift, axis=1) if shift else block
            out = moved if out is None else jnp.where(quarter == i, moved, out)
        return out

    for g in range(GROUPS):
        info = [ext_ref[4 * g + i, :, 128:].astype(F32) for i in range(4)]
        ids, gates = gather(info, 0), gather(info, 1)
        named = jnp.zeros((PEERS, 128), F32)
        dense = jnp.zeros((PEERS, 128), F32)
        for k in range(8):
            hit = ids[k : k + 1, :] == expert
            named = jnp.where(hit, 1.0, named)
            dense = jnp.where(hit, gates[k : k + 1, :], dense)
        rank = dot(named.astype(BF16), ahead, 1, 0)
        code_ref[g] = jnp.where(named > 0.5, rank, -1.0)
        gate_ref[g] = dense
        cols = [ext_ref[4 * g + i, :, :128].astype(F32) for i in range(4)]
        for h in range(4):
            cols_ref[h * 8 : (h + 1) * 8, g * 128 : (g + 1) * 128] = gather(cols, h)


def input_kernel(me_ref, s_ref, code_ref, gate_ref, og_ref, rw_ref, ready_ref, out_ref, tie_ref):
    del ready_ref
    me = me_ref[0]
    mine = s_ref[pl.ds(me // 16, PEERS, stride=4), :]
    offset = ((me // 4) % 4) * 32 + (me % 4) * CAP
    mine = pltpu.roll(mine, (128 - offset) % 128, axis=1)
    code = code_ref[...]
    sdg = jnp.zeros((PEERS, TOK), F32)
    for c in range(CAP):
        sdg = jnp.where(code == c, mine[:, c : c + 1], sdg)
    total = jnp.sum(sdg, axis=0, keepdims=True)
    logit_grad = (sdg - gate_ref[...] * total).astype(BF16)
    part = dot(logit_grad, rw_ref[...], 0, 0)
    out_ref[...] = (og_ref[...].astype(F32) + part).astype(BF16)
    tie_ref[...] = total[:, :1] + jnp.zeros((8, 128), F32)


def router_kernel(s_ref, code_ref, gate_ref, cols_ref, spread_ref, tie_ref, out_ref, lg_ref):
    del tie_ref
    lane = iota((PEERS, 128), 1)
    for t in range(4):
        tile = s_ref[pl.ds(t, PEERS, stride=4), :]
        for q in range(4):
            g = t * 4 + q
            x = pltpu.roll(tile, 128 - 32 * q, axis=1) if q else tile
            x = jnp.where(lane < 24, x, 0.0)
            hi = x.astype(BF16).astype(F32)
            rest = x - hi
            mid = rest.astype(BF16).astype(F32)
            low = (rest - mid).astype(BF16).astype(F32)
            z = hi + pltpu.roll(mid, 32, axis=1) + pltpu.roll(low, 64, axis=1)
            wide = dot(z.astype(BF16), spread_ref[...], 1, 0)
            code = code_ref[g]
            sdg = jnp.zeros((PEERS, 128), F32)
            for c in range(CAP):
                sdg = jnp.where(code == c, wide[:, c * 128 : (c + 1) * 128], sdg)
            total = jnp.sum(sdg, axis=0, keepdims=True)
            lg_ref[:, g * 128 : (g + 1) * 128] = (sdg - gate_ref[g] * total).astype(BF16)
    out_ref[...] = dot(cols_ref[...].astype(BF16), lg_ref[...], 1, 1)


def call(kernel, outs, scratch=(), flops=0, moved=0, **kw):
    return pl.pallas_call(
        kernel,
        out_shape=outs,
        scratch_shapes=list(scratch),
        compiler_params=pltpu.CompilerParams(vmem_limit_bytes=32 << 20),
        cost_estimate=pl.CostEstimate(flops=flops, bytes_accessed=moved, transcendentals=0),
        **kw,
    )


def whole():
    return pl.BlockSpec(memory_space=pltpu.VMEM)


def struct(shape, dtype):
    return jax.ShapeDtypeStruct(shape, dtype)


def pack(og, li, rw, ids):
    return call(
        pack_kernel,
        (
            struct((PEERS, CHUNK, WIDE), BF16),
            struct((PEERS, TOK), F32),
            struct((PEERS, TOK), F32),
        ),
        [pltpu.VMEM((PEERS, WIDE), F32), pltpu.VMEM((PEERS, WIDE), F32)],
        flops=10**9,
        moved=2 * 10**6,
        name="pack",
    )(og, li, rw, ids)


def expert(recv, w, h, perm):
    return call(
        expert_kernel,
        (struct((SLOTS, SLOTS), BF16), struct((PEERS * 4, 128), F32)),
        [pltpu.VMEM((SLOTS, PARTS * WIDE), BF16)],
        flops=12 * 10**8,
        moved=4 * 10**6,
        grid=(1,),
        in_specs=[
            pl.BlockSpec((PEERS, ROWS, WIDE), lambda i: (0, 0, 0)),
            pl.BlockSpec(w.shape, lambda i: (0, 0)),
            pl.BlockSpec(h.shape, lambda i: (0, 0)),
            pl.BlockSpec(perm.shape, lambda i: (0, 0)),
        ],
        out_specs=(
            pl.BlockSpec((SLOTS, SLOTS), lambda i: (0, 0)),
            pl.BlockSpec((PEERS * 4, 128), lambda i: (0, 0)),
        ),
        name="expert",
    )(recv, w, h, perm)


def side(recv, sdg):
    return call(
        side_kernel,
        (
            struct((GROUPS, PEERS, 128), F32),
            struct((GROUPS, PEERS, 128), F32),
            struct((TOK, PEERS * TOK), F32),
            struct((8, 128), F32),
        ),
        flops=10**8,
        moved=2 * 10**6,
        grid=(1,),
        in_specs=[
            pl.BlockSpec((PEERS, 8, WIDE), lambda i: (0, ROWS // 8, 0)),
            pl.BlockSpec((8, 128), lambda i: (0, 0)),
        ],
        out_specs=(
            pl.BlockSpec((GROUPS, PEERS, 128), lambda i: (0, 0, 0)),
            pl.BlockSpec((GROUPS, PEERS, 128), lambda i: (0, 0, 0)),
            pl.BlockSpec((TOK, PEERS * TOK), lambda i: (0, 0)),
            pl.BlockSpec((8, 128), lambda i: (0, 0)),
        ),
        name="side",
    )(recv, sdg)


def input_grads(me, s, code, gate, og, rw, ready):
    return call(
        input_kernel,
        (struct(og.shape, BF16), struct((8, 128), F32)),
        flops=10**7,
        moved=10**6,
        in_specs=[pl.BlockSpec(memory_space=pltpu.SMEM)] + [whole()] * 6,
        name="inputs",
    )(me, s, code, gate, og, rw, ready)


def router_grads(s, code, gate, cols, spread, tie):
    return call(
        router_kernel,
        struct((TOK, PEERS), F32),
        [pltpu.VMEM((PEERS, PEERS * TOK), BF16)],
        flops=3 * 10**8,
        moved=2 * 10**6,
        name="router",
    )(s, code, gate, cols, spread, tie)


def exchange(x):
    return lax.all_to_all(x, "expert", split_axis=0, concat_axis=0, tiled=True)


def shards(out_grad, layer_input, router_weight, expert_ids, hidden_act, down_weight):
    og, li = out_grad[0], layer_input[0]
    rw = jnp.swapaxes(router_weight[0], 0, 1)
    ids = jnp.swapaxes(expert_ids[0], 0, 1)
    me = lax.axis_index("expert").astype(jnp.int32).reshape(1)
    send, gate, code = pack(og, li, rw, ids)
    recv = exchange(send)
    hidden_grad, sdg = expert(
        recv, down_weight[0, 0], hidden_act[0, 0], jnp.asarray(compaction(), BF16)
    )
    back = exchange(sdg.reshape(PEERS, 4, 128)).reshape(PEERS * 4, 128)
    all_gate, all_code, cols, ready = side(recv, sdg)
    input_grad, tie = input_grads(me, back, code, gate, og, rw, ready)
    sections = lax.axis_size("section")
    sent = lax.ppermute(
        input_grad[None], "section", [(i, (i - 1) % sections) for i in range(sections)]
    )
    router_grad = router_grads(
        back, all_code, all_gate, cols, jnp.asarray(spreading(), BF16), tie
    )
    return sent, hidden_grad[None, None], router_grad[None]


def solution(mesh):
    placed = (
        P("section", "expert", None),
        P("section", "expert", None),
        P("section", None, None),
        P("section", "expert", None),
        P("section", "expert", None, None),
        P("section", "expert", None, None),
    )
    return jax.shard_map(
        shards,
        mesh=mesh,
        in_specs=placed,
        out_specs=(
            P("section", "expert", None),
            P("section", "expert", None, None),
            P("section", "expert", None),
        ),
        check_vma=False,
    )
```

time: 294 us -> 107 us (0.36); the launches traced: 290 us -> 107 us
  waiting for transfers between devices: 205 us -> 8.84 us
  blocking collectives: 0 us -> 63.1 us
  starting transfers between devices: 40.3 us -> 18 us
  between operations: 14.2 us -> 0.75 us
  local copies, waits for them, and re-layouts: 17.4 us -> 7.47 us
  Pallas kernels: 0 us -> 8.65 us
  matrix products: 7.04 us -> 0 us
  other arithmetic: 5.85 us -> 0 us
    unnamed x2 -> x0, waiting for transfers between devices: 145 us -> none
    all_to_all x0 -> x1, blocking collectives: none -> 63.1 us  [exchange(): return lax.all_to_all(x, 'expert', split_axis=0, concat_axis=0, tiled=True)]
    all_to_all x3 -> x1, waiting for transfers between devices: 59.7 us -> 8.84 us  [exchange(): return lax.all_to_all(x, 'expert', split_axis=0, concat_axis=0, tiled=True)]
    all_to_all x3 -> x1, starting transfers between devices: 29.7 us -> 6.22 us  [exchange(): return lax.all_to_all(x, 'expert', split_axis=0, concat_axis=0, tiled=True)]
    pallas_call x0 -> x5, Pallas kernels: none -> 8.65 us  [the longest x1 2.55 us: expert(): call(expert_kernel, (struct((SLOTS, SLOTS), BF16), struct((PEERS * 4, 128...]
    dot_general x7 -> x0, matrix products: 7.04 us -> none  [the longest x1 2.95 us: shards(): expert_out = jnp.dot(hidden, w_down, preferred_element_type=jnp.float32)]
    convert_element_type x4 -> x0, local copies, waits for them, and re-layouts: 6.76 us -> none  [the longest x1 4 us: shards(): slot_dg = jnp.sum(slot_rows.astype(jnp.float32) * expert_out, axis=-1)]
    convert_element_type x4 -> x0, other arithmetic: 3.42 us -> none  [the longest x1 3.37 us: shards(): scaled = (recv_gates.reshape(-1).astype(jnp.float32)[:, None] * slot_rows...]
  transfers between devices with their start and end apart: 5 -> 2, of which waited for: 3 -> 1; matrix products, arithmetic and copies ran while one was open for 4% -> 0% of each run, Pallas kernels for 0% -> 3%
where the time goes in v1:
time: 107 us
  blocking collectives  63.1 us (59%)
  starting transfers between devices  18 us (17%)
  waiting for transfers between devices  8.84 us (8%)
  Pallas kernels  8.65 us (8%)
  local copies, waits for them, and re-layouts  7.47 us (7%)
    all_to_all x1, blocking collectives, exchange(): return lax.all_to_all(x, 'expert', split_axis=0, concat_axis=0, tiled=True)  63.1 us
    ppermute x1, starting transfers between devices, shards(): lax.ppermute(input_grad[None], 'section', [(i, (i - 1) % sections) for i...  11.8 us
    all_to_all x1, waiting for transfers between devices, exchange(): return lax.all_to_all(x, 'expert', split_axis=0, concat_axis=0, tiled=True)  8.84 us
    unnamed x29, local copies, waits for them, and re-layouts  7.47 us
    all_to_all x1, starting transfers between devices, exchange(): return lax.all_to_all(x, 'expert', split_axis=0, concat_axis=0, tiled=True)  6.22 us
    pallas_call x1, Pallas kernels, expert(): call(expert_kernel, (struct((SLOTS, SLOTS), BF16), struct((PEERS * 4, 128...  2.55 us
    pallas_call x1, Pallas kernels, pack(): call(pack_kernel, (struct((PEERS, CHUNK, WIDE), BF16), struct((PEERS, TOK...  2.34 us
  transfers between devices with their start and end apart: 2, of which 1 were waited for; matrix products, arithmetic and copies ran while one was open for 0% of the time, Pallas kernels for 3%

profile of v1, /device:TPU:1, one launch (start us, length us, event | category | flops | bytes accessed | tf_op | source)
XLA Modules:
  0.0 106.8 jit_solution(13988517791513225115)
XLA Ops:
  0.6 0.0 copy-start
  0.6 0.9 copy-done
  1.6 0.0 copy-start.3
  1.6 0.9 copy-done.3
  2.5 0.0 copy-start.11
  2.5 0.9 copy-done.11
  3.4 0.0 copy-start.12
  3.4 0.7 copy-done.12
  4.1 2.3 %pack.1 = (bf16[64,56,256]{2,1,0:T(8,128)(2,1)S(1)}, f32[64,32]{1,0:T(8,128)S(1)}, f32[64,32]{1,0:T(8,128)S(1)}) custom-call(bf16[32,2048]{1,0:T(8,128)(2,1)S(1)} %bitcast.20, bf16[32,2048]{1,0:T(8,128)(2,1)S(1)} %bitcast.24, bf16[64,2048]{1,0:T(8,128)(2,1)S(1)} %bitcast.18, s32[8,32]{1,0:T(8,128)S(1)} %bitcast.26), custom_call_target="tpu_custom_call" | custom-call | flops 1000000000 | bytes 2000000 | tf_op jit(solution)/shard_map/pack/pallas_call | solution.py:233
  6.4 0.0 copy-start.5
  6.4 0.0 copy-start.7
  6.4 0.0 copy-start.9
  6.5 0.0 copy-start.10
  6.5 0.0 copy-start.13
  6.5 63.1 %all_to_all.10.recv_ref.ext_ref = bf16[64,56,256]{2,1,0:T(8,128)(2,1)S(1)} all-to-all(bf16[64,56,256]{2,1,0:T(8,128)(2,1)S(1)} %get-tuple-element.14), channel_id=1, replica_groups=mesh['section'=16,'expert'=64] {'expert'}, dimensions={0} | all-to-all | bytes 3670016 | tf_op jit(solution)/shard_map/all_to_all | solution.py:318
  69.6 0.0 copy-done.5
  69.6 0.0 copy-done.7
  69.6 0.0 copy-done.9
  69.6 0.0 copy-done.10
  69.6 0.0 copy-done.13
  69.6 2.5 %expert.1 = (bf16[384,384]{1,0:T(8,128)(2,1)}, f32[256,128]{1,0:T(8,128)}) custom-call(bf16[64,56,256]{2,1,0:T(8,128)(2,1)S(1)} %all_to_all.10.recv_ref.ext_ref, bf16[384,2048]{1,0:T(8,128)(2,1)S(1)} %bitcast.22, bf16[384,384]{1,0:T(8,128)(2,1)S(1)} %bitcast.23, bf16[384,384]{1,0:T(8,128)(2,1)S(1)} %copy-done.13), custom_call_target="tpu_custom_call" | custom-call | flops 1200000000 | bytes 4000000 | tf_op jit(solution)/shard_map/expert/pallas_call | solution.py:248
  72.1 0.0 copy-start.1
  72.1 6.2 %all-to-all-start.1 = ((f32[64,4,128]{2,1,0:T(4,128)}), f32[64,4,128]{2,1,0:T(4,128)S(1)}, u32[]{:S(2)}, u32[]{:S(2)}) async-start(f32[64,4,128]{2,1,0:T(4,128)} %bitcast.9), calls=%async_computation.1 | async-start | bytes 262144 | tf_op jit(solution)/shard_map/all_to_all | solution.py:318
  78.4 1.5 %side.1 = (f32[16,64,128]{2,1,0:T(8,128)S(1)}, f32[16,64,128]{2,1,0:T(8,128)S(1)}, f32[32,2048]{1,0:T(8,128)S(1)}, f32[8,128]{1,0:T(8,128)S(1)}) custom-call(bf16[64,56,256]{2,1,0:T(8,128)(2,1)S(1)} %all_to_all.10.recv_ref.ext_ref, f32[256,128]{1,0:T(8,128)} %get-tuple-element.15.sdg_ref), custom_call_target="tpu_custom_call" | custom-call | flops 100000000 | bytes 2000000 | tf_op jit(solution)/shard_map/side/pallas_call | solution.py:270
  79.9 8.8 %all-to-all-done.1 = f32[64,4,128]{2,1,0:T(4,128)S(1)} async-done(((f32[64,4,128]{2,1,0:T(4,128)}), f32[64,4,128]{2,1,0:T(4,128)S(1)}, u32[]{:S(2)}, u32[]{:S(2)}) %all-to-all-start.1) | async-done | bytes 131104 | tf_op jit(solution)/shard_map/all_to_all | solution.py:318
  88.7 0.0 copy-done.1
  88.7 0.0 copy-start.4
  88.7 0.9 copy-done.4
  89.6 0.0 copy-start.6
  89.6 0.8 copy-done.6
  90.4 0.0 copy-start.8
  90.4 0.8 copy-done.8
  91.2 0.4 inputs.1
  91.6 11.8 %collective-permute-start = (bf16[1,32,2048]{2,1,0:T(8,128)(2,1)S(1)}, bf16[1,32,2048]{2,1,0:T(8,128)(2,1)S(1)}, u32[]{:S(2)}, u32[]{:S(2)}) collective-permute-start(bf16[1,32,2048]{2,1,0:T(8,128)(2,1)S(1)} %bitcast.25), channel_id=1, source_target_pairs={{0,960},{64,0},{128,64},{192,128},{256,192},{320,256},{384,320},{4... | collective-permute-start | bytes 393224 | tf_op jit(solution)/shard_map/ppermute | solution.py:335
  103.4 0.0 copy-start.2
  103.4 0.9 copy-done.2
  104.4 1.8 %router.1 = f32[32,64]{1,0:T(8,128)} custom-call(f32[256,128]{1,0:T(8,128)S(1)} %bitcast.17, f32[16,64,128]{2,1,0:T(8,128)S(1)} %get-tuple-element.21.code_ref, f32[16,64,128]{2,1,0:T(8,128)S(1)} %get-tuple-element.22.gate_ref, f32[32,2048]{1,0:T(8,128)S(1)} %get-tuple-element.23.cols_ref, bf16[128,768]{1,0:T(8,128)(2,1)S(1)} %copy-done.2, ...), custom_call_target="tpu_custom_call" | custom-call | flops 300000000 | bytes 2000000 | tf_op jit(solution)/shard_map/router/pallas_call | solution.py:307
  106.2 0.0 collective-permute-done
  106.2 0.7 copy.12
Async XLA Ops:
  0.6 1.0 copy-start
  1.6 0.9 copy-start.3
  2.5 0.9 copy-start.11
  3.4 0.7 copy-start.12
  6.4 63.1 %copy-start.5 = (f32[64,32]{1,0:T(8,128)}, f32[64,32]{1,0:T(8,128)S(1)}, u32[]{:S(2)}) copy-start(f32[64,32]{1,0:T(8,128)S(1)} %get-tuple-element.17.gate_ref) | copy-start | bytes 24580
  6.4 63.1 %copy-start.7 = (f32[64,32]{1,0:T(8,128)}, f32[64,32]{1,0:T(8,128)S(1)}, u32[]{:S(2)}) copy-start(f32[64,32]{1,0:T(8,128)S(1)} %get-tuple-element.16.code_ref) | copy-start | bytes 24580
  6.4 63.1 %copy-start.9 = (bf16[1,1,384,2048]{3,2,1,0:T(8,128)(2,1)S(1)}, bf16[1,1,384,2048]{3,2,1,0:T(8,128)(2,1)}, u32[]{:S(2)}) copy-start(bf16[1,1,384,2048]{3,2,1,0:T(8,128)(2,1)} %param.13) | copy-start | bytes 4718596
  6.5 63.1 %copy-start.10 = (bf16[1,1,384,384]{3,2,1,0:T(8,128)(2,1)S(1)}, bf16[1,1,384,384]{3,2,1,0:T(8,128)(2,1)}, u32[]{:S(2)}) copy-start(bf16[1,1,384,384]{3,2,1,0:T(8,128)(2,1)} %param.12) | copy-start | bytes 884740
  6.5 63.1 %copy-start.13 = (bf16[384,384]{1,0:T(8,128)(2,1)S(1)}, bf16[384,384]{1,0:T(8,128)(2,1)}, u32[]{:S(2)}) copy-start(bf16[384,384]{1,0:T(8,128)(2,1)} %constant.8.clone.perm_ref) | copy-start | bytes 884740
  72.1 16.6 %copy-start.1 = (bf16[1,2048,64]{1,2,0:T(8,128)(2,1)S(1)}, bf16[1,2048,64]{1,2,0:T(8,128)(2,1)}, u32[]{:S(2)}) copy-start(bf16[1,2048,64]{1,2,0:T(8,128)(2,1)} %param.10) | copy-start | bytes 786436
  72.1 16.6 %all-to-all-start.1 = ((f32[64,4,128]{2,1,0:T(4,128)}), f32[64,4,128]{2,1,0:T(4,128)S(1)}, u32[]{:S(2)}, u32[]{:S(2)}) async-start(f32[64,4,128]{2,1,0:T(4,128)} %bitcast.9), calls=%async_computation.1 | async-start | bytes 262144 | tf_op jit(solution)/shard_map/all_to_all | solution.py:318
  88.7 0.9 copy-start.4
  89.6 0.8 copy-start.6
  90.4 0.8 copy-start.8
  91.6 14.6 %collective-permute-start = (bf16[1,32,2048]{2,1,0:T(8,128)(2,1)S(1)}, bf16[1,32,2048]{2,1,0:T(8,128)(2,1)S(1)}, u32[]{:S(2)}, u32[]{:S(2)}) collective-permute-start(bf16[1,32,2048]{2,1,0:T(8,128)(2,1)S(1)} %bitcast.25), channel_id=1, source_target_pairs={{0,960},{64,0},{128,64},{192,128},{256,192},{320,256},{384,320},{4... | collective-permute-start | bytes 393224 | tf_op jit(solution)/shard_map/ppermute | solution.py:335
  103.4 0.9 copy-start.2

commit v2 on v1

--- a/solution.py
+++ b/solution.py
@@ -37,17 +37,23 @@
 
 
 def spreading():
-    m = np.zeros((128, CAP * 128), np.float32)
-    for piece in range(3):
-        for b in range(4):
-            for c in range(CAP):
-                row = piece * 32 + b * CAP + c
-                m[row, c * 128 + b * TOK : c * 128 + (b + 1) * TOK] = 1
-    return m
-
-
-def pack_kernel(og_ref, li_ref, rw_ref, ids_ref, send_ref, gate_ref, code_ref, gt_ref, ct_ref):
+    row, lane = iota((128, CAP * 128), 0), iota((128, CAP * 128), 1)
+    slot = ((lane // TOK) & 3) * CAP + lane // 128
+    return jnp.where(((row & 31) == slot) & (row < 96), 1.0, 0.0).astype(BF16)
+
+
+def pack_kernel(
+    og_hbm, li_hbm, rw_hbm, ids_hbm, send_ref, gate_ref, code_ref,
+    og_ref, li_ref, rw_ref, ids_ref, gt_ref, ct_ref, sems,
+):
+    pairs = ((ids_hbm, ids_ref), (rw_hbm, rw_ref), (li_hbm, li_ref), (og_hbm, og_ref))
+    copies = [pltpu.make_async_copy(a, b, sems.at[i]) for i, (a, b) in enumerate(pairs)]
+    for copy in copies:
+        copy.start()
+    copies[0].wait()
     ids = ids_ref[...]
+    copies[1].wait()
+    copies[2].wait()
     logits = dot(rw_ref[...], li_ref[...], 1, 1)
     expert = iota((PEERS, TOK), 0)
     named = jnp.zeros((PEERS, TOK), F32)
@@ -87,6 +93,7 @@
         columns = jnp.where(quarter == h, spread[:, h], columns)
     send_ref[:, ROWS:, :128] = columns.astype(BF16)
 
+    copies[3].wait()
     stacked = jnp.concatenate(
         [og_ref[:, j * WIDE : (j + 1) * WIDE] for j in range(PARTS)], axis=0
     )
@@ -169,8 +176,16 @@
             cols_ref[h * 8 : (h + 1) * 8, g * 128 : (g + 1) * 128] = gather(cols, h)
 
 
-def input_kernel(me_ref, s_ref, code_ref, gate_ref, og_ref, rw_ref, ready_ref, out_ref, tie_ref):
+def input_kernel(
+    me_ref, s_ref, code_ref, gate_ref, ready_ref, og_hbm, rw_hbm, out_ref, tie_ref, og_ref, rw_ref, sems
+):
     del ready_ref
+    copies = [
+        pltpu.make_async_copy(rw_hbm, rw_ref, sems.at[0]),
+        pltpu.make_async_copy(og_hbm, og_ref, sems.at[1]),
+    ]
+    for copy in copies:
+        copy.start()
     me = me_ref[0]
     mine = s_ref[pl.ds(me // 16, PEERS, stride=4), :]
     offset = ((me // 4) % 4) * 32 + (me % 4) * CAP
@@ -181,13 +196,16 @@
         sdg = jnp.where(code == c, mine[:, c : c + 1], sdg)
     total = jnp.sum(sdg, axis=0, keepdims=True)
     logit_grad = (sdg - gate_ref[...] * total).astype(BF16)
+    for copy in copies:
+        copy.wait()
     part = dot(logit_grad, rw_ref[...], 0, 0)
     out_ref[...] = (og_ref[...].astype(F32) + part).astype(BF16)
     tie_ref[...] = total[:, :1] + jnp.zeros((8, 128), F32)
 
 
-def router_kernel(s_ref, code_ref, gate_ref, cols_ref, spread_ref, tie_ref, out_ref, lg_ref):
+def router_kernel(s_ref, code_ref, gate_ref, cols_ref, tie_ref, out_ref, spread_ref, lg_ref):
     del tie_ref
+    spread_ref[...] = spreading()
     lane = iota((PEERS, 128), 1)
     for t in range(4):
         tile = s_ref[pl.ds(t, PEERS, stride=4), :]
@@ -215,7 +233,7 @@
         kernel,
         out_shape=outs,
         scratch_shapes=list(scratch),
-        compiler_params=pltpu.CompilerParams(vmem_limit_bytes=32 << 20),
+        compiler_params=pltpu.CompilerParams(vmem_limit_bytes=kw.pop("limit", 32) << 20),
         cost_estimate=pl.CostEstimate(flops=flops, bytes_accessed=moved, transcendentals=0),
         **kw,
     )
@@ -223,6 +241,10 @@
 
 def whole():
     return pl.BlockSpec(memory_space=pltpu.VMEM)
+
+
+def far():
+    return pl.BlockSpec(memory_space=pltpu.HBM)
 
 
 def struct(shape, dtype):
@@ -237,9 +259,12 @@
             struct((PEERS, TOK), F32),
             struct((PEERS, TOK), F32),
         ),
-        [pltpu.VMEM((PEERS, WIDE), F32), pltpu.VMEM((PEERS, WIDE), F32)],
+        [pltpu.VMEM(a.shape, a.dtype) for a in (og, li, rw, ids)]
+        + [pltpu.VMEM((PEERS, WIDE), F32)] * 2
+        + [pltpu.SemaphoreType.DMA((4,))],
         flops=10**9,
         moved=2 * 10**6,
+        in_specs=[far()] * 4,
         name="pack",
     )(og, li, rw, ids)
 
@@ -267,14 +292,15 @@
 
 
 def side(recv, sdg):
+    outs = (
+        struct((GROUPS, PEERS, 128), F32),
+        struct((GROUPS, PEERS, 128), F32),
+        struct((TOK, PEERS * TOK), F32),
+        struct((8, 128), F32),
+    )
     return call(
         side_kernel,
-        (
-            struct((GROUPS, PEERS, 128), F32),
-            struct((GROUPS, PEERS, 128), F32),
-            struct((TOK, PEERS * TOK), F32),
-            struct((8, 128), F32),
-        ),
+        outs,
         flops=10**8,
         moved=2 * 10**6,
         grid=(1,),
@@ -282,36 +308,32 @@
             pl.BlockSpec((PEERS, 8, WIDE), lambda i: (0, ROWS // 8, 0)),
             pl.BlockSpec((8, 128), lambda i: (0, 0)),
         ],
-        out_specs=(
-            pl.BlockSpec((GROUPS, PEERS, 128), lambda i: (0, 0, 0)),
-            pl.BlockSpec((GROUPS, PEERS, 128), lambda i: (0, 0, 0)),
-            pl.BlockSpec((TOK, PEERS * TOK), lambda i: (0, 0)),
-            pl.BlockSpec((8, 128), lambda i: (0, 0)),
-        ),
+        out_specs=tuple(whole() for _ in outs),
         name="side",
     )(recv, sdg)
 
 
-def input_grads(me, s, code, gate, og, rw, ready):
+def input_grads(me, s, code, gate, ready, og, rw):
     return call(
         input_kernel,
         (struct(og.shape, BF16), struct((8, 128), F32)),
+        [pltpu.VMEM(a.shape, a.dtype) for a in (og, rw)] + [pltpu.SemaphoreType.DMA((2,))],
         flops=10**7,
         moved=10**6,
-        in_specs=[pl.BlockSpec(memory_space=pltpu.SMEM)] + [whole()] * 6,
+        in_specs=[pl.BlockSpec(memory_space=pltpu.SMEM)] + [whole()] * 4 + [far()] * 2,
         name="inputs",
-    )(me, s, code, gate, og, rw, ready)
-
-
-def router_grads(s, code, gate, cols, spread, tie):
+    )(me, s, code, gate, ready, og, rw)
+
+
+def router_grads(s, code, gate, cols, tie):
     return call(
         router_kernel,
         struct((TOK, PEERS), F32),
-        [pltpu.VMEM((PEERS, PEERS * TOK), BF16)],
+        [pltpu.VMEM((128, CAP * 128), BF16), pltpu.VMEM((PEERS, PEERS * TOK), BF16)],
         flops=3 * 10**8,
         moved=2 * 10**6,
         name="router",
-    )(s, code, gate, cols, spread, tie)
+    )(s, code, gate, cols, tie)
 
 
 def exchange(x):
@@ -322,6 +344,9 @@
     og, li = out_grad[0], layer_input[0]
     rw = jnp.swapaxes(router_weight[0], 0, 1)
     ids = jnp.swapaxes(expert_ids[0], 0, 1)
+    og, li, rw, ids = [
+        pltpu.with_memory_space_constraint(a, pltpu.HBM) for a in (og, li, rw, ids)
+    ]
     me = lax.axis_index("expert").astype(jnp.int32).reshape(1)
     send, gate, code = pack(og, li, rw, ids)
     recv = exchange(send)
@@ -330,14 +355,12 @@
     )
     back = exchange(sdg.reshape(PEERS, 4, 128)).reshape(PEERS * 4, 128)
     all_gate, all_code, cols, ready = side(recv, sdg)
-    input_grad, tie = input_grads(me, back, code, gate, og, rw, ready)
+    input_grad, tie = input_grads(me, back, code, gate, ready, og, rw)
     sections = lax.axis_size("section")
     sent = lax.ppermute(
         input_grad[None], "section", [(i, (i - 1) % sections) for i in range(sections)]
     )
-    router_grad = router_grads(
-        back, all_code, all_gate, cols, jnp.asarray(spreading(), BF16), tie
-    )
+    router_grad = router_grads(back, all_code, all_gate, cols, tie)
     return sent, hidden_grad[None, None], router_grad[None]
 
 

time: 107 us -> 103 us (0.963)
  local copies, waits for them, and re-layouts: 7.47 us -> 0.67 us
  Pallas kernels: 8.65 us -> 10.5 us
    unnamed x29 -> x7, local copies, waits for them, and re-layouts: 7.47 us -> 0.67 us
  transfers between devices with their start and end apart: 2 -> 2, of which waited for: 1 -> 2; matrix products, arithmetic and copies ran while one was open for 0% -> 0% of each run, Pallas kernels for 3% -> 3%
where the time goes in v2:
time: 103 us; the launch traced here: 102 us
  blocking collectives  63.1 us (61%)
  starting transfers between devices  17.9 us (17%)
  Pallas kernels  10.5 us (10%)
  waiting for transfers between devices  9.51 us (9%)
    all_to_all x1, blocking collectives, exchange(): return lax.all_to_all(x, 'expert', split_axis=0, concat_axis=0, tiled=True)  63.1 us
    ppermute x1, starting transfers between devices, shards(): lax.ppermute(input_grad[None], 'section', [(i, (i - 1) % sections) for i...  11.8 us
    all_to_all x1, waiting for transfers between devices, exchange(): return lax.all_to_all(x, 'expert', split_axis=0, concat_axis=0, tiled=True)  8.84 us
    all_to_all x1, starting transfers between devices, exchange(): return lax.all_to_all(x, 'expert', split_axis=0, concat_axis=0, tiled=True)  6.09 us
    pallas_call x1, Pallas kernels, pack(): call(pack_kernel, (struct((PEERS, CHUNK, WIDE), BF16), struct((PEERS, TOK...  3.39 us
    pallas_call x1, Pallas kernels, expert(): call(expert_kernel, (struct((SLOTS, SLOTS), BF16), struct((PEERS * 4, 128...  2.54 us
  transfers between devices with their start and end apart: 2, of which 2 were waited for; matrix products, arithmetic and copies ran while one was open for 0% of the time, Pallas kernels for 3%

profile of v2, /device:TPU:1, one launch (start us, length us, event | category | flops | bytes accessed | tf_op | source)
XLA Modules:
  0.0 102.3 jit_solution(845880759886272778)
XLA Ops:
  0.6 3.4 %pack.1 = (bf16[64,56,256]{2,1,0:T(8,128)(2,1)S(1)}, f32[64,32]{1,0:T(8,128)S(1)}, f32[64,32]{1,0:T(8,128)S(1)}) custom-call(bf16[32,2048]{1,0:T(8,128)(2,1)} %bitcast.23, bf16[32,2048]{1,0:T(8,128)(2,1)} %bitcast.26, bf16[64,2048]{1,0:T(8,128)(2,1)} %bitcast.21, s32[8,32]{1,0:T(8,128)} %bitcast.27), custom_call_target="tpu_custom_call" | custom-call | flops 1000000000 | bytes 2000000 | tf_op jit(solution)/shard_map/pack/pallas_call | solution.py:255
  4.0 0.0 copy-start
  4.0 0.0 copy-start.1
  4.1 0.0 copy-start.2
  4.1 63.1 %all_to_all.10.recv_ref.ext_ref = bf16[64,56,256]{2,1,0:T(8,128)(2,1)S(1)} all-to-all(bf16[64,56,256]{2,1,0:T(8,128)(2,1)S(1)} %get-tuple-element.14), channel_id=1, replica_groups=mesh['section'=16,'expert'=64] {'expert'}, dimensions={0} | all-to-all | bytes 3670016 | tf_op jit(solution)/shard_map/all_to_all | solution.py:340
  67.1 0.0 copy-done
  67.1 0.0 copy-done.1
  67.1 0.0 copy-done.2
  67.1 2.5 %expert.1 = (bf16[384,384]{1,0:T(8,128)(2,1)}, f32[256,128]{1,0:T(8,128)}) custom-call(bf16[64,56,256]{2,1,0:T(8,128)(2,1)S(1)} %all_to_all.10.recv_ref.ext_ref, bf16[384,2048]{1,0:T(8,128)(2,1)S(1)} %bitcast.18, bf16[384,384]{1,0:T(8,128)(2,1)S(1)} %bitcast.19, bf16[384,384]{1,0:T(8,128)(2,1)S(1)} %copy-done.2), custom_call_target="tpu_custom_call" | custom-call | flops 1200000000 | bytes 4000000 | tf_op jit(solution)/shard_map/expert/pallas_call | solution.py:273
  69.7 6.1 %all-to-all-start.1 = ((f32[64,4,128]{2,1,0:T(4,128)}), f32[64,4,128]{2,1,0:T(4,128)S(1)}, u32[]{:S(2)}, u32[]{:S(2)}) async-start(f32[64,4,128]{2,1,0:T(4,128)} %bitcast.9), calls=%async_computation.1 | async-start | bytes 262144 | tf_op jit(solution)/shard_map/all_to_all | solution.py:340
  75.8 1.5 %side.1 = (f32[16,64,128]{2,1,0:T(8,128)S(1)}, f32[16,64,128]{2,1,0:T(8,128)S(1)}, f32[32,2048]{1,0:T(8,128)S(1)}, f32[8,128]{1,0:T(8,128)S(1)}) custom-call(bf16[64,56,256]{2,1,0:T(8,128)(2,1)S(1)} %all_to_all.10.recv_ref.ext_ref, f32[256,128]{1,0:T(8,128)} %get-tuple-element.15.sdg_ref), custom_call_target="tpu_custom_call" | custom-call | flops 100000000 | bytes 2000000 | tf_op jit(solution)/shard_map/side/pallas_call | solution.py:301
  77.3 8.8 %all-to-all-done.1 = f32[64,4,128]{2,1,0:T(4,128)S(1)} async-done(((f32[64,4,128]{2,1,0:T(4,128)}), f32[64,4,128]{2,1,0:T(4,128)S(1)}, u32[]{:S(2)}, u32[]{:S(2)}) %all-to-all-start.1) | async-done | bytes 131104 | tf_op jit(solution)/shard_map/all_to_all | solution.py:340
  86.2 1.2 %inputs.1 = (bf16[32,2048]{1,0:T(8,128)(2,1)S(1)}, f32[8,128]{1,0:T(8,128)S(1)}) custom-call(s32[1]{0:T(128)} %bitcast.me_ref, f32[256,128]{1,0:T(8,128)S(1)} %bitcast.16, f32[64,32]{1,0:T(8,128)S(1)} %get-tuple-element.16.code_ref, f32[64,32]{1,0:T(8,128)S(1)} %get-tuple-element.17.gate_ref, f32[8,128]{1,0:T(8,128)S(1)} %get-tuple-element.18.ready_ref, ...), custom_call_target="tpu_custom_call" | custom-call | flops 10000000 | bytes 1000000 | tf_op jit(solution)/shard_map/inputs/pallas_call | solution.py:317
  87.4 11.8 %collective-permute-start = (bf16[1,32,2048]{2,1,0:T(8,128)(2,1)S(1)}, bf16[1,32,2048]{2,1,0:T(8,128)(2,1)S(1)}, u32[]{:S(2)}, u32[]{:S(2)}) collective-permute-start(bf16[1,32,2048]{2,1,0:T(8,128)(2,1)S(1)} %bitcast.20), channel_id=1, source_target_pairs={{0,960},{64,0},{128,64},{192,128},{256,192},{320,256},{384,320},{4... | collective-permute-start | bytes 393224 | tf_op jit(solution)/shard_map/ppermute | solution.py:360
  99.2 1.8 %router.1 = f32[32,64]{1,0:T(8,128)} custom-call(f32[256,128]{1,0:T(8,128)S(1)} %bitcast.17, f32[16,64,128]{2,1,0:T(8,128)S(1)} %get-tuple-element.21.code_ref, f32[16,64,128]{2,1,0:T(8,128)S(1)} %get-tuple-element.22.gate_ref, f32[32,2048]{1,0:T(8,128)S(1)} %get-tuple-element.23.cols_ref, f32[8,128]{1,0:T(8,128)S(1)} %get-tuple-element.24.tie_ref), custom_call_target="tpu_custom_call" | custom-call | flops 300000000 | bytes 2000000 | tf_op jit(solution)/shard_map/router/pallas_call | solution.py:329
  101.0 0.7 collective-permute-done
  101.7 0.7 copy.11
Async XLA Ops:
  4.0 63.1 %copy-start = (bf16[1,1,384,2048]{3,2,1,0:T(8,128)(2,1)S(1)}, bf16[1,1,384,2048]{3,2,1,0:T(8,128)(2,1)}, u32[]{:S(2)}) copy-start(bf16[1,1,384,2048]{3,2,1,0:T(8,128)(2,1)} %param.12) | copy-start | bytes 4718596
  4.0 63.1 %copy-start.1 = (bf16[1,1,384,384]{3,2,1,0:T(8,128)(2,1)S(1)}, bf16[1,1,384,384]{3,2,1,0:T(8,128)(2,1)}, u32[]{:S(2)}) copy-start(bf16[1,1,384,384]{3,2,1,0:T(8,128)(2,1)} %param.11) | copy-start | bytes 884740
  4.1 63.1 %copy-start.2 = (bf16[384,384]{1,0:T(8,128)(2,1)S(1)}, bf16[384,384]{1,0:T(8,128)(2,1)}, u32[]{:S(2)}) copy-start(bf16[384,384]{1,0:T(8,128)(2,1)} %constant.6.clone.perm_ref) | copy-start | bytes 884740
  69.7 16.5 %all-to-all-start.1 = ((f32[64,4,128]{2,1,0:T(4,128)}), f32[64,4,128]{2,1,0:T(4,128)S(1)}, u32[]{:S(2)}, u32[]{:S(2)}) async-start(f32[64,4,128]{2,1,0:T(4,128)} %bitcast.9), calls=%async_computation.1 | async-start | bytes 262144 | tf_op jit(solution)/shard_map/all_to_all | solution.py:340
  87.4 14.3 %collective-permute-start = (bf16[1,32,2048]{2,1,0:T(8,128)(2,1)S(1)}, bf16[1,32,2048]{2,1,0:T(8,128)(2,1)S(1)}, u32[]{:S(2)}, u32[]{:S(2)}) collective-permute-start(bf16[1,32,2048]{2,1,0:T(8,128)(2,1)S(1)} %bitcast.20), channel_id=1, source_target_pairs={{0,960},{64,0},{128,64},{192,128},{256,192},{320,256},{384,320},{4... | collective-permute-start | bytes 393224 | tf_op jit(solution)/shard_map/ppermute | solution.py:360

commit v3 on v2

--- a/solution.py
+++ b/solution.py
@@ -28,11 +28,11 @@
 
 
 def compaction():
-    p = np.zeros((8 * ROWS, 8 * ROWS), np.float32)
+    p = np.zeros((4 * ROWS, 4 * ROWS), np.float32)
     for part in range(PARTS):
-        for b in range(8):
+        for b in range(4):
             for c in range(CAP):
-                p[part * ROWS + b * CAP + c, b * ROWS + part * CAP + c] = 1
+                p[part * 4 * CAP + b * CAP + c, b * ROWS + part * CAP + c] = 1
     return p
 
 
@@ -43,7 +43,7 @@
 
 
 def pack_kernel(
-    og_hbm, li_hbm, rw_hbm, ids_hbm, send_ref, gate_ref, code_ref,
+    og_hbm, li_hbm, rw_hbm, ids_hbm, send_ref,
     og_ref, li_ref, rw_ref, ids_ref, gt_ref, ct_ref, sems,
 ):
     pairs = ((ids_hbm, ids_ref), (rw_hbm, rw_ref), (li_hbm, li_ref), (og_hbm, og_ref))
@@ -52,15 +52,10 @@
         copy.start()
     copies[0].wait()
     ids = ids_ref[...]
-    copies[1].wait()
-    copies[2].wait()
-    logits = dot(rw_ref[...], li_ref[...], 1, 1)
     expert = iota((PEERS, TOK), 0)
     named = jnp.zeros((PEERS, TOK), F32)
     for k in range(8):
         named = jnp.where(ids[k : k + 1, :] == expert, 1.0, named)
-    weights = jnp.where(named > 0.5, jnp.exp(logits), 0.0)
-    gates = (weights / jnp.sum(weights, axis=0, keepdims=True)).astype(BF16)
     token = iota((TOK, WIDE), 0)
     lane = iota((TOK, WIDE), 1) & (TOK - 1)
     tile = jnp.where(token == lane, 1.0, 0.0).astype(BF16)
@@ -68,10 +63,13 @@
     named_b = named.astype(BF16)
     code = jnp.where(dot(named_b, tile, 1, 0) > 0.5, dot(named_b, ahead, 1, 0), -1.0)
     ct_ref[...] = code
+    copies[1].wait()
+    copies[2].wait()
+    logits = dot(rw_ref[...], li_ref[...], 1, 1)
+    weights = jnp.where(named > 0.5, jnp.exp(logits), 0.0)
+    gates = (weights / jnp.sum(weights, axis=0, keepdims=True)).astype(BF16)
     gt_ref[...] = dot(gates, tile, 1, 0)
     gates_f = gates.astype(F32)
-    gate_ref[...] = gates_f
-    code_ref[...] = code[:, :TOK]
 
     choice = iota((8, TOK), 0)
     compact = jnp.zeros((8, TOK), F32)
@@ -121,12 +119,14 @@
 def expert_kernel(recv_ref, w_ref, h_ref, perm_ref, hg_ref, sdg_ref, rows_ref):
     perm = perm_ref[...]
     for g in range(8):
-        chunk = recv_ref[g * 8 : (g + 1) * 8, :, :].reshape(8 * ROWS, WIDE)
-        moved = dot(perm, chunk, 1, 0).astype(BF16)
+        halves = []
+        for h in range(2):
+            b = g * 8 + h * 4
+            chunk = recv_ref[b : b + 4, :ROWS, :].reshape(4 * ROWS, WIDE)
+            halves.append(dot(perm, chunk, 1, 0))
         for j in range(PARTS):
-            rows_ref[g * ROWS : (g + 1) * ROWS, j * WIDE : (j + 1) * WIDE] = moved[
-                j * ROWS : (j + 1) * ROWS
-            ]
+            piece = jnp.concatenate([m[j * 24 : (j + 1) * 24] for m in halves], axis=0)
+            rows_ref[g * ROWS : (g + 1) * ROWS, j * WIDE : (j + 1) * WIDE] = piece.astype(BF16)
     grad = dot(rows_ref[...], w_ref[...], 1, 1)
     hg_ref[...] = grad.astype(BF16)
     prod = grad * h_ref[...].astype(F32)
@@ -144,8 +144,8 @@
     sdg_ref[...] = jnp.broadcast_to(out[None], (PEERS // 2, 8, 128)).reshape(PEERS * 4, 128)
 
 
-def side_kernel(ext_ref, sdg_ref, gate_ref, code_ref, cols_ref, ready_ref):
-    ready_ref[...] = sdg_ref[...]
+def side_kernel(recv_ref, sdg_ref, gate_ref, code_ref, cols_ref, ready_ref):
+    ready_ref[...] = sdg_ref[:8, :]
     expert = iota((PEERS, 128), 0).astype(F32)
     row, col = iota((128, 128), 0), iota((128, 128), 1)
     ahead = jnp.where((row // TOK == col // TOK) & (row < col), 1.0, 0.0).astype(BF16)
@@ -160,7 +160,7 @@
         return out
 
     for g in range(GROUPS):
-        info = [ext_ref[4 * g + i, :, 128:].astype(F32) for i in range(4)]
+        info = [recv_ref[4 * g + i, ROWS:, 128:].astype(F32) for i in range(4)]
         ids, gates = gather(info, 0), gather(info, 1)
         named = jnp.zeros((PEERS, 128), F32)
         dense = jnp.zeros((PEERS, 128), F32)
@@ -171,36 +171,29 @@
         rank = dot(named.astype(BF16), ahead, 1, 0)
         code_ref[g] = jnp.where(named > 0.5, rank, -1.0)
         gate_ref[g] = dense
-        cols = [ext_ref[4 * g + i, :, :128].astype(F32) for i in range(4)]
+        cols = [recv_ref[4 * g + i, ROWS:, :128].astype(F32) for i in range(4)]
         for h in range(4):
             cols_ref[h * 8 : (h + 1) * 8, g * 128 : (g + 1) * 128] = gather(cols, h)
 
 
-def input_kernel(
-    me_ref, s_ref, code_ref, gate_ref, ready_ref, og_hbm, rw_hbm, out_ref, tie_ref, og_ref, rw_ref, sems
-):
-    del ready_ref
-    copies = [
-        pltpu.make_async_copy(rw_hbm, rw_ref, sems.at[0]),
-        pltpu.make_async_copy(og_hbm, og_ref, sems.at[1]),
-    ]
-    for copy in copies:
-        copy.start()
+def logit_kernel(me_ref, s_ref, code_ref, gate_ref, out_ref):
     me = me_ref[0]
     mine = s_ref[pl.ds(me // 16, PEERS, stride=4), :]
     offset = ((me // 4) % 4) * 32 + (me % 4) * CAP
     mine = pltpu.roll(mine, (128 - offset) % 128, axis=1)
-    code = code_ref[...]
+    back = (128 - (me % 4) * TOK) % 128
+    code = pltpu.roll(code_ref[me // 4], back, axis=1)[:, :TOK]
+    gate = pltpu.roll(gate_ref[me // 4], back, axis=1)[:, :TOK]
     sdg = jnp.zeros((PEERS, TOK), F32)
     for c in range(CAP):
         sdg = jnp.where(code == c, mine[:, c : c + 1], sdg)
     total = jnp.sum(sdg, axis=0, keepdims=True)
-    logit_grad = (sdg - gate_ref[...] * total).astype(BF16)
-    for copy in copies:
-        copy.wait()
-    part = dot(logit_grad, rw_ref[...], 0, 0)
+    out_ref[...] = (sdg - gate * total).astype(BF16)
+
+
+def input_kernel(lg_ref, og_ref, rw_ref, out_ref):
+    part = dot(lg_ref[...], rw_ref[...], 0, 0)
     out_ref[...] = (og_ref[...].astype(F32) + part).astype(BF16)
-    tie_ref[...] = total[:, :1] + jnp.zeros((8, 128), F32)
 
 
 def router_kernel(s_ref, code_ref, gate_ref, cols_ref, tie_ref, out_ref, spread_ref, lg_ref):
@@ -254,11 +247,7 @@
 def pack(og, li, rw, ids):
     return call(
         pack_kernel,
-        (
-            struct((PEERS, CHUNK, WIDE), BF16),
-            struct((PEERS, TOK), F32),
-            struct((PEERS, TOK), F32),
-        ),
+        struct((PEERS, CHUNK, WIDE), BF16),
         [pltpu.VMEM(a.shape, a.dtype) for a in (og, li, rw, ids)]
         + [pltpu.VMEM((PEERS, WIDE), F32)] * 2
         + [pltpu.SemaphoreType.DMA((4,))],
@@ -276,17 +265,6 @@
         [pltpu.VMEM((SLOTS, PARTS * WIDE), BF16)],
         flops=12 * 10**8,
         moved=4 * 10**6,
-        grid=(1,),
-        in_specs=[
-            pl.BlockSpec((PEERS, ROWS, WIDE), lambda i: (0, 0, 0)),
-            pl.BlockSpec(w.shape, lambda i: (0, 0)),
-            pl.BlockSpec(h.shape, lambda i: (0, 0)),
-            pl.BlockSpec(perm.shape, lambda i: (0, 0)),
-        ],
-        out_specs=(
-            pl.BlockSpec((SLOTS, SLOTS), lambda i: (0, 0)),
-            pl.BlockSpec((PEERS * 4, 128), lambda i: (0, 0)),
-        ),
         name="expert",
     )(recv, w, h, perm)
 
@@ -303,26 +281,29 @@
         outs,
         flops=10**8,
         moved=2 * 10**6,
-        grid=(1,),
-        in_specs=[
-            pl.BlockSpec((PEERS, 8, WIDE), lambda i: (0, ROWS // 8, 0)),
-            pl.BlockSpec((8, 128), lambda i: (0, 0)),
-        ],
-        out_specs=tuple(whole() for _ in outs),
         name="side",
     )(recv, sdg)
 
 
-def input_grads(me, s, code, gate, ready, og, rw):
+def logit_grads(me, s, code, gate):
+    return call(
+        logit_kernel,
+        struct((PEERS, TOK), BF16),
+        flops=10**6,
+        moved=2 * 10**5,
+        in_specs=[pl.BlockSpec(memory_space=pltpu.SMEM)] + [whole()] * 3,
+        name="logits",
+    )(me, s, code, gate)
+
+
+def input_grads(lg, og, rw):
     return call(
         input_kernel,
-        (struct(og.shape, BF16), struct((8, 128), F32)),
-        [pltpu.VMEM(a.shape, a.dtype) for a in (og, rw)] + [pltpu.SemaphoreType.DMA((2,))],
+        struct(og.shape, BF16),
         flops=10**7,
         moved=10**6,
-        in_specs=[pl.BlockSpec(memory_space=pltpu.SMEM)] + [whole()] * 4 + [far()] * 2,
         name="inputs",
-    )(me, s, code, gate, ready, og, rw)
+    )(lg, og, rw)
 
 
 def router_grads(s, code, gate, cols, tie):
@@ -336,6 +317,11 @@
     )(s, code, gate, cols, tie)
 
 
+def shifted(x):
+    n = lax.axis_size("section")
+    return lax.ppermute(x, "section", [(i, (i - 1) % n) for i in range(n)])
+
+
 def exchange(x):
     return lax.all_to_all(x, "expert", split_axis=0, concat_axis=0, tiled=True)
 
@@ -344,23 +330,21 @@
     og, li = out_grad[0], layer_input[0]
     rw = jnp.swapaxes(router_weight[0], 0, 1)
     ids = jnp.swapaxes(expert_ids[0], 0, 1)
-    og, li, rw, ids = [
-        pltpu.with_memory_space_constraint(a, pltpu.HBM) for a in (og, li, rw, ids)
-    ]
+    far_args = [pltpu.with_memory_space_constraint(a, pltpu.HBM) for a in (og, li, rw, ids)]
     me = lax.axis_index("expert").astype(jnp.int32).reshape(1)
-    send, gate, code = pack(og, li, rw, ids)
+    send = pack(*far_args)
     recv = exchange(send)
     hidden_grad, sdg = expert(
         recv, down_weight[0, 0], hidden_act[0, 0], jnp.asarray(compaction(), BF16)
     )
     back = exchange(sdg.reshape(PEERS, 4, 128)).reshape(PEERS * 4, 128)
     all_gate, all_code, cols, ready = side(recv, sdg)
-    input_grad, tie = input_grads(me, back, code, gate, ready, og, rw)
-    sections = lax.axis_size("section")
-    sent = lax.ppermute(
-        input_grad[None], "section", [(i, (i - 1) % sections) for i in range(sections)]
-    )
-    router_grad = router_grads(back, all_code, all_gate, cols, tie)
+    og_held, rw_held, _ = lax.optimization_barrier((og, rw, ready))
+    og_next, rw_next = shifted(og_held), shifted(rw_held)
+    logit_grad = logit_grads(me, back, all_code, all_gate)
+    logit_next = shifted(logit_grad)
+    router_grad = router_grads(back, all_code, all_gate, cols, logit_grad)
+    sent = input_grads(logit_next, og_next, rw_next)[None]
     return sent, hidden_grad[None, None], router_grad[None]
 
 

time: 103 us -> 102 us (level)
  waiting for transfers between devices: 9.51 us -> 0.01 us
  starting transfers between devices: 17.9 us -> 26 us
  Pallas kernels: 10.5 us -> 11.6 us
    all_to_all x1, waiting for transfers between devices: 8.84 us -> 0.01 us  [exchange(): return lax.all_to_all(x, 'expert', split_axis=0, concat_axis=0, tiled=True)]
    ppermute x1 -> x3, starting transfers between devices: 11.8 us -> 19.9 us  [shifted(): return lax.ppermute(x, 'section', [(i, (i - 1) % n) for i in range(n)])]
    pallas_call x3 -> x4, Pallas kernels: 6.13 us -> 7.65 us  [the longest x1 3.4 us: pack(): call(pack_kernel, struct((PEERS, CHUNK, WIDE), BF16), [pltpu.VMEM(a.shape...]
  transfers between devices with their start and end apart: 2 -> 4, of which waited for: 2 -> 0; matrix products, arithmetic and copies ran while one was open for 0% -> 0% of each run, Pallas kernels for 3% -> 4%
where the time goes in v3:
time: 102 us; the launch traced here: 101 us
  blocking collectives  63.1 us (62%)
  starting transfers between devices  26 us (25%)
  Pallas kernels  11.6 us (11%)
    all_to_all x1, blocking collectives, exchange(): return lax.all_to_all(x, 'expert', split_axis=0, concat_axis=0, tiled=True)  63.1 us
    ppermute x3, starting transfers between devices, shifted(): return lax.ppermute(x, 'section', [(i, (i - 1) % n) for i in range(n)])  19.9 us
    all_to_all x1, starting transfers between devices, exchange(): return lax.all_to_all(x, 'expert', split_axis=0, concat_axis=0, tiled=True)  6.09 us
    pallas_call x1, Pallas kernels, pack(): call(pack_kernel, struct((PEERS, CHUNK, WIDE), BF16), [pltpu.VMEM(a.shape...  3.4 us
    pallas_call x1, Pallas kernels, side(): call(side_kernel, outs, flops=10 ** 8, moved=2 * 10 ** 6, name='side')  2.24 us
    pallas_call x1, Pallas kernels, expert(): call(expert_kernel, (struct((SLOTS, SLOTS), BF16), struct((PEERS * 4, 128...  2.15 us
  transfers between devices with their start and end apart: 4, of which 0 were waited for; matrix products, arithmetic and copies ran while one was open for 0% of the time, Pallas kernels for 4%

profile of v3, /device:TPU:1, one launch (start us, length us, event | category | flops | bytes accessed | tf_op | source)
XLA Modules:
  0.0 101.4 jit_solution(12671699875621384829)
XLA Ops:
  0.6 3.4 %pack.1 = bf16[64,56,256]{2,1,0:T(8,128)(2,1)S(1)} custom-call(bf16[32,2048]{1,0:T(8,128)(2,1)} %bitcast.1.og_hbm, bf16[32,2048]{1,0:T(8,128)(2,1)} %bitcast.22, bf16[64,2048]{1,0:T(8,128)(2,1)} %bitcast.4.rw_hbm, s32[8,32]{1,0:T(8,128)} %bitcast.23), custom_call_target="tpu_custom_call" | custom-call | flops 1000000000 | bytes 2000000 | tf_op jit(solution)/shard_map/pack/pallas_call | solution.py:248
  4.0 0.0 copy-start
  4.0 0.0 copy-start.1
  4.1 0.0 copy-start.2
  4.1 63.1 %all_to_all.10.recv_ref = bf16[64,56,256]{2,1,0:T(8,128)(2,1)S(1)} all-to-all(bf16[64,56,256]{2,1,0:T(8,128)(2,1)S(1)} %pack.1), channel_id=1, replica_groups=mesh['section'=16,'expert'=64] {'expert'}, dimensions={0} | all-to-all | bytes 3670016 | tf_op jit(solution)/shard_map/all_to_all | solution.py:326
  67.1 0.0 copy-done
  67.1 0.0 copy-done.1
  67.2 0.0 copy-done.2
  67.2 2.1 %expert.1 = (bf16[384,384]{1,0:T(8,128)(2,1)}, f32[256,128]{1,0:T(8,128)}) custom-call(bf16[64,56,256]{2,1,0:T(8,128)(2,1)S(1)} %all_to_all.10.recv_ref, bf16[384,2048]{1,0:T(8,128)(2,1)S(1)} %bitcast.18, bf16[384,384]{1,0:T(8,128)(2,1)S(1)} %bitcast.19, bf16[192,192]{1,0:T(8,128)(2,1)S(1)} %copy-done.2), custom_call_target="tpu_custom_call" | custom-call | flops 1200000000 | bytes 4000000 | tf_op jit(solution)/shard_map/expert/pallas_call | solution.py:262
  69.3 6.1 %all-to-all-start.1 = ((f32[64,4,128]{2,1,0:T(4,128)}), f32[64,4,128]{2,1,0:T(4,128)S(1)}, u32[]{:S(2)}, u32[]{:S(2)}) async-start(f32[64,4,128]{2,1,0:T(4,128)} %bitcast.9), calls=%async_computation.1 | async-start | bytes 262144 | tf_op jit(solution)/shard_map/all_to_all | solution.py:326
  75.4 11.8 %collective-permute-start.2 = (bf16[64,2048]{1,0:T(8,128)(2,1)}, bf16[64,2048]{1,0:T(8,128)(2,1)S(1)}, u32[]{:S(2)}, u32[]{:S(2)}) collective-permute-start(bf16[64,2048]{1,0:T(8,128)(2,1)} %bitcast.4.rw_hbm), channel_id=1, source_target_pairs={{0,960},{64,0},{128,64},{192,128},{256,192},{320,256},{384,320},{4... | collective-permute-start | bytes 786440 | tf_op jit(solution)/shard_map/ppermute | solution.py:322
  87.2 2.2 %collective-permute-start.1 = (bf16[32,2048]{1,0:T(8,128)(2,1)}, bf16[32,2048]{1,0:T(8,128)(2,1)}, u32[]{:S(2)}, u32[]{:S(2)}) collective-permute-start(bf16[32,2048]{1,0:T(8,128)(2,1)} %bitcast.1.og_hbm), channel_id=1, source_target_pairs={{0,960},{64,0},{128,64},{192,128},{256,192},{320,256},{384,320},{4... | collective-permute-start | bytes 393224 | tf_op jit(solution)/shard_map/ppermute | solution.py:322
  89.4 2.2 %side.1 = (f32[16,64,128]{2,1,0:T(8,128)S(1)}, f32[16,64,128]{2,1,0:T(8,128)S(1)}, f32[32,2048]{1,0:T(8,128)S(1)}, f32[8,128]{1,0:T(8,128)}) custom-call(bf16[64,56,256]{2,1,0:T(8,128)(2,1)S(1)} %all_to_all.10.recv_ref, f32[256,128]{1,0:T(8,128)} %get-tuple-element.10.sdg_ref), custom_call_target="tpu_custom_call" | custom-call | flops 100000000 | bytes 2000000 | tf_op jit(solution)/shard_map/side/pallas_call | solution.py:279
  91.7 0.0 all-to-all-done.1
  91.7 0.2 logits.1.tie_ref
  91.9 5.9 %collective-permute-start = (bf16[64,32]{1,0:T(8,128)(2,1)S(1)}, bf16[64,32]{1,0:T(8,128)(2,1)S(1)}, u32[]{:S(2)}, u32[]{:S(2)}) collective-permute-start(bf16[64,32]{1,0:T(8,128)(2,1)S(1)} %logits.1.tie_ref), channel_id=1, source_target_pairs={{0,960},{64,0},{128,64},{192,128},{256,192},{320,256},{384,320},{4... | collective-permute-start | bytes 12296 | tf_op jit(solution)/shard_map/ppermute | solution.py:322
  97.8 1.8 %router.1 = f32[32,64]{1,0:T(8,128)} custom-call(f32[256,128]{1,0:T(8,128)S(1)} %bitcast.17, f32[16,64,128]{2,1,0:T(8,128)S(1)} %get-tuple-element.11.code_ref, f32[16,64,128]{2,1,0:T(8,128)S(1)} %get-tuple-element.12.gate_ref, f32[32,2048]{1,0:T(8,128)S(1)} %get-tuple-element.16.cols_ref, bf16[64,32]{1,0:T(8,128)(2,1)S(1)} %logits.1.tie_ref), custom_call_target="tpu_custom_call" | custom-call | flops 300000000 | bytes 2000000 | tf_op jit(solution)/shard_map/router/pallas_call | solution.py:310
  99.6 0.0 collective-permute-done.1.og_ref
  99.6 0.0 collective-permute-done.2.rw_ref
  99.6 0.0 collective-permute-done.lg_ref
  99.6 1.8 %inputs.1 = bf16[32,2048]{1,0:T(8,128)(2,1)} custom-call(bf16[64,32]{1,0:T(8,128)(2,1)S(1)} %collective-permute-done.lg_ref, bf16[32,2048]{1,0:T(8,128)(2,1)} %collective-permute-done.1.og_ref, bf16[64,2048]{1,0:T(8,128)(2,1)S(1)} %collective-permute-done.2.rw_ref), custom_call_target="tpu_custom_call" | custom-call | flops 10000000 | bytes 1000000 | tf_op jit(solution)/shard_map/inputs/pallas_call | solution.py:300
Async XLA Ops:
  4.0 63.1 %copy-start = (bf16[1,1,384,2048]{3,2,1,0:T(8,128)(2,1)S(1)}, bf16[1,1,384,2048]{3,2,1,0:T(8,128)(2,1)}, u32[]{:S(2)}) copy-start(bf16[1,1,384,2048]{3,2,1,0:T(8,128)(2,1)} %param.12) | copy-start | bytes 4718596
  4.0 63.1 %copy-start.1 = (bf16[1,1,384,384]{3,2,1,0:T(8,128)(2,1)S(1)}, bf16[1,1,384,384]{3,2,1,0:T(8,128)(2,1)}, u32[]{:S(2)}) copy-start(bf16[1,1,384,384]{3,2,1,0:T(8,128)(2,1)} %param.11) | copy-start | bytes 884740
  4.1 63.1 %copy-start.2 = (bf16[192,192]{1,0:T(8,128)(2,1)S(1)}, bf16[192,192]{1,0:T(8,128)(2,1)}, u32[]{:S(2)}) copy-start(bf16[192,192]{1,0:T(8,128)(2,1)} %constant.6.clone.perm_ref) | copy-start | bytes 221188
  69.3 22.4 %all-to-all-start.1 = ((f32[64,4,128]{2,1,0:T(4,128)}), f32[64,4,128]{2,1,0:T(4,128)S(1)}, u32[]{:S(2)}, u32[]{:S(2)}) async-start(f32[64,4,128]{2,1,0:T(4,128)} %bitcast.9), calls=%async_computation.1 | async-start | bytes 262144 | tf_op jit(solution)/shard_map/all_to_all | solution.py:326
  75.4 24.2 %collective-permute-start.2 = (bf16[64,2048]{1,0:T(8,128)(2,1)}, bf16[64,2048]{1,0:T(8,128)(2,1)S(1)}, u32[]{:S(2)}, u32[]{:S(2)}) collective-permute-start(bf16[64,2048]{1,0:T(8,128)(2,1)} %bitcast.4.rw_hbm), channel_id=1, source_target_pairs={{0,960},{64,0},{128,64},{192,128},{256,192},{320,256},{384,320},{4... | collective-permute-start | bytes 786440 | tf_op jit(solution)/shard_map/ppermute | solution.py:322
  87.2 12.4 %collective-permute-start.1 = (bf16[32,2048]{1,0:T(8,128)(2,1)}, bf16[32,2048]{1,0:T(8,128)(2,1)}, u32[]{:S(2)}, u32[]{:S(2)}) collective-permute-start(bf16[32,2048]{1,0:T(8,128)(2,1)} %bitcast.1.og_hbm), channel_id=1, source_target_pairs={{0,960},{64,0},{128,64},{192,128},{256,192},{320,256},{384,320},{4... | collective-permute-start | bytes 393224 | tf_op jit(solution)/shard_map/ppermute | solution.py:322
  91.9 7.7 %collective-permute-start = (bf16[64,32]{1,0:T(8,128)(2,1)S(1)}, bf16[64,32]{1,0:T(8,128)(2,1)S(1)}, u32[]{:S(2)}, u32[]{:S(2)}) collective-permute-start(bf16[64,32]{1,0:T(8,128)(2,1)S(1)} %logits.1.tie_ref), channel_id=1, source_target_pairs={{0,960},{64,0},{128,64},{192,128},{256,192},{320,256},{384,320},{4... | collective-permute-start | bytes 12296 | tf_op jit(solution)/shard_map/ppermute | solution.py:322

commit v4 on v3

--- a/solution.py
+++ b/solution.py
@@ -43,8 +43,7 @@
 
 
 def pack_kernel(
-    og_hbm, li_hbm, rw_hbm, ids_hbm, send_ref,
-    og_ref, li_ref, rw_ref, ids_ref, gt_ref, ct_ref, sems,
+    og_hbm, li_hbm, rw_hbm, ids_hbm, send_ref, og_ref, li_ref, rw_ref, ids_ref, gt_ref, ct_ref, sems
 ):
     pairs = ((ids_hbm, ids_ref), (rw_hbm, rw_ref), (li_hbm, li_ref), (og_hbm, og_ref))
     copies = [pltpu.make_async_copy(a, b, sems.at[i]) for i, (a, b) in enumerate(pairs)]
@@ -113,7 +112,7 @@
         send_ref[pl.ds(i * 8, 8), :ROWS, :] = rows.reshape(8, ROWS, WIDE)
         return carry
 
-    lax.fori_loop(0, PEERS // 8, step, 0)
+    lax.fori_loop(0, PEERS // 8, step, 0, unroll=8)
 
 
 def expert_kernel(recv_ref, w_ref, h_ref, perm_ref, hg_ref, sdg_ref, rows_ref):
@@ -144,21 +143,22 @@
     sdg_ref[...] = jnp.broadcast_to(out[None], (PEERS // 2, 8, 128)).reshape(PEERS * 4, 128)
 
 
-def side_kernel(recv_ref, sdg_ref, gate_ref, code_ref, cols_ref, ready_ref):
-    ready_ref[...] = sdg_ref[:8, :]
+def gather(blocks, at):
+    quarter = iota((8, 128), 1) // TOK
+    out = None
+    for i, block in enumerate(blocks):
+        shift = (i - at) * TOK % 128
+        moved = pltpu.roll(block, shift, axis=1) if shift else block
+        out = moved if out is None else jnp.where(quarter == i, moved, out)
+    return out
+
+
+def side_kernel(recv_ref, hg_ref, gate_ref, code_ref, hg_hbm, sem):
+    copy = pltpu.make_async_copy(hg_ref, hg_hbm, sem)
+    copy.start()
     expert = iota((PEERS, 128), 0).astype(F32)
     row, col = iota((128, 128), 0), iota((128, 128), 1)
     ahead = jnp.where((row // TOK == col // TOK) & (row < col), 1.0, 0.0).astype(BF16)
-    quarter = iota((8, 128), 1) // TOK
-
-    def gather(blocks, at):
-        out = None
-        for i, block in enumerate(blocks):
-            shift = (i - at) * TOK % 128
-            moved = pltpu.roll(block, shift, axis=1) if shift else block
-            out = moved if out is None else jnp.where(quarter == i, moved, out)
-        return out
-
     for g in range(GROUPS):
         info = [recv_ref[4 * g + i, ROWS:, 128:].astype(F32) for i in range(4)]
         ids, gates = gather(info, 0), gather(info, 1)
@@ -171,9 +171,7 @@
         rank = dot(named.astype(BF16), ahead, 1, 0)
         code_ref[g] = jnp.where(named > 0.5, rank, -1.0)
         gate_ref[g] = dense
-        cols = [recv_ref[4 * g + i, ROWS:, :128].astype(F32) for i in range(4)]
-        for h in range(4):
-            cols_ref[h * 8 : (h + 1) * 8, g * 128 : (g + 1) * 128] = gather(cols, h)
+    copy.wait()
 
 
 def logit_kernel(me_ref, s_ref, code_ref, gate_ref, out_ref):
@@ -191,14 +189,39 @@
     out_ref[...] = (sdg - gate * total).astype(BF16)
 
 
-def input_kernel(lg_ref, og_ref, rw_ref, out_ref):
-    part = dot(lg_ref[...], rw_ref[...], 0, 0)
-    out_ref[...] = (og_ref[...].astype(F32) + part).astype(BF16)
-
-
-def router_kernel(s_ref, code_ref, gate_ref, cols_ref, tie_ref, out_ref, spread_ref, lg_ref):
+def input_kernel(lg_ref, og_hbm, rw_hbm, out_hbm, og_ref, rw_ref, out_ref, sems):
+    spans = [pl.ds(i * 512, 512) for i in range(4)]
+    loads = [
+        pltpu.make_async_copy(rw_hbm.at[:, at], rw_ref.at[:, at], sems.at[i])
+        for i, at in enumerate(spans)
+    ] + [pltpu.make_async_copy(og_hbm, og_ref, sems.at[8])]
+    stores = [
+        pltpu.make_async_copy(out_ref.at[:, at], out_hbm.at[:, at], sems.at[4 + i])
+        for i, at in enumerate(spans)
+    ]
+    for copy in loads:
+        copy.start()
+    lg = lg_ref[...]
+    for i, at in enumerate(spans):
+        loads[i].wait()
+        part = dot(lg, rw_ref[:, at], 0, 0)
+        if i == 0:
+            loads[4].wait()
+        out_ref[:, at] = (og_ref[:, at].astype(F32) + part).astype(BF16)
+        stores[i].start()
+    for copy in stores:
+        copy.wait()
+
+
+def router_kernel(
+    s_ref, code_ref, gate_ref, recv_ref, tie_ref, out_ref, cols_ref, spread_ref, lg_ref
+):
     del tie_ref
     spread_ref[...] = spreading()
+    for g in range(GROUPS):
+        cols = [recv_ref[4 * g + i, ROWS:, :128].astype(F32) for i in range(4)]
+        for h in range(4):
+            cols_ref[h * 8 : (h + 1) * 8, g * 128 : (g + 1) * 128] = gather(cols, h)
     lane = iota((PEERS, 128), 1)
     for t in range(4):
         tile = s_ref[pl.ds(t, PEERS, stride=4), :]
@@ -269,20 +292,20 @@
     )(recv, w, h, perm)
 
 
-def side(recv, sdg):
-    outs = (
-        struct((GROUPS, PEERS, 128), F32),
-        struct((GROUPS, PEERS, 128), F32),
-        struct((TOK, PEERS * TOK), F32),
-        struct((8, 128), F32),
-    )
+def side(recv, hg):
     return call(
         side_kernel,
-        outs,
+        (
+            struct((GROUPS, PEERS, 128), F32),
+            struct((GROUPS, PEERS, 128), F32),
+            struct(hg.shape, BF16),
+        ),
+        [pltpu.SemaphoreType.DMA],
         flops=10**8,
         moved=2 * 10**6,
+        out_specs=(whole(), whole(), far()),
         name="side",
-    )(recv, sdg)
+    )(recv, hg)
 
 
 def logit_grads(me, s, code, gate):
@@ -300,21 +323,28 @@
     return call(
         input_kernel,
         struct(og.shape, BF16),
+        [pltpu.VMEM(a.shape, BF16) for a in (og, rw, og)] + [pltpu.SemaphoreType.DMA((9,))],
         flops=10**7,
         moved=10**6,
+        in_specs=[whole(), far(), far()],
+        out_specs=far(),
         name="inputs",
     )(lg, og, rw)
 
 
-def router_grads(s, code, gate, cols, tie):
+def router_grads(s, code, gate, recv, tie):
     return call(
         router_kernel,
         struct((TOK, PEERS), F32),
-        [pltpu.VMEM((128, CAP * 128), BF16), pltpu.VMEM((PEERS, PEERS * TOK), BF16)],
+        [
+            pltpu.VMEM((TOK, PEERS * TOK), F32),
+            pltpu.VMEM((128, CAP * 128), BF16),
+            pltpu.VMEM((PEERS, PEERS * TOK), BF16),
+        ],
         flops=3 * 10**8,
         moved=2 * 10**6,
         name="router",
-    )(s, code, gate, cols, tie)
+    )(s, code, gate, recv, tie)
 
 
 def shifted(x):
@@ -334,16 +364,16 @@
     me = lax.axis_index("expert").astype(jnp.int32).reshape(1)
     send = pack(*far_args)
     recv = exchange(send)
-    hidden_grad, sdg = expert(
+    hidden_near, sdg = expert(
         recv, down_weight[0, 0], hidden_act[0, 0], jnp.asarray(compaction(), BF16)
     )
     back = exchange(sdg.reshape(PEERS, 4, 128)).reshape(PEERS * 4, 128)
-    all_gate, all_code, cols, ready = side(recv, sdg)
-    og_held, rw_held, _ = lax.optimization_barrier((og, rw, ready))
+    og_held, rw_held, sdg = lax.optimization_barrier((og, rw, sdg))
     og_next, rw_next = shifted(og_held), shifted(rw_held)
+    all_gate, all_code, hidden_grad = side(recv, hidden_near)
     logit_grad = logit_grads(me, back, all_code, all_gate)
     logit_next = shifted(logit_grad)
-    router_grad = router_grads(back, all_code, all_gate, cols, logit_grad)
+    router_grad = router_grads(back, all_code, all_gate, recv, logit_grad)
     sent = input_grads(logit_next, og_next, rw_next)[None]
     return sent, hidden_grad[None, None], router_grad[None]
 

time: 102 us -> 101 us (level)
  Pallas kernels: 11.6 us -> 9.43 us
  starting transfers between devices: 26 us -> 27.5 us
    ppermute x3, starting transfers between devices: 19.9 us -> 21.4 us  [shifted(): return lax.ppermute(x, 'section', [(i, (i - 1) % n) for i in range(n)])]
    pallas_call x3, Pallas kernels: 5.81 us -> 4.64 us  [the longest x1 2.12 us: input_grads(): call(input_kernel, struct(og.shape, BF16), [pltpu.VMEM(a.shape, BF16) for...]
  transfers between devices with their start and end apart: 4 -> 4, of which waited for: 0 -> 0; matrix products, arithmetic and copies ran while one was open for 0% -> 0% of each run, Pallas kernels for 4% -> 3%
where the time goes in v4:
time: 101 us
  blocking collectives  63.1 us (62%)
  starting transfers between devices  27.5 us (27%)
  Pallas kernels  9.43 us (9%)
    all_to_all x1, blocking collectives, exchange(): return lax.all_to_all(x, 'expert', split_axis=0, concat_axis=0, tiled=True)  63.1 us
    ppermute x3, starting transfers between devices, shifted(): return lax.ppermute(x, 'section', [(i, (i - 1) % n) for i in range(n)])  21.4 us
    all_to_all x1, starting transfers between devices, exchange(): return lax.all_to_all(x, 'expert', split_axis=0, concat_axis=0, tiled=True)  6.09 us
    pallas_call x1, Pallas kernels, pack(): call(pack_kernel, struct((PEERS, CHUNK, WIDE), BF16), [pltpu.VMEM(a.shape...  2.41 us
    pallas_call x1, Pallas kernels, expert(): call(expert_kernel, (struct((SLOTS, SLOTS), BF16), struct((PEERS * 4, 128...  2.15 us
    pallas_call x1, Pallas kernels, input_grads(): call(input_kernel, struct(og.shape, BF16), [pltpu.VMEM(a.shape, BF16) for...  2.12 us
  transfers between devices with their start and end apart: 4, of which 0 were waited for; matrix products, arithmetic and copies ran while one was open for 0% of the time, Pallas kernels for 3%

profile of v4, /device:TPU:1, one launch (start us, length us, event | category | flops | bytes accessed | tf_op | source)
XLA Modules:
  0.0 100.8 jit_solution(7602370443266644497)
XLA Ops:
  0.6 2.4 %pack.1 = bf16[64,56,256]{2,1,0:T(8,128)(2,1)S(1)} custom-call(bf16[32,2048]{1,0:T(8,128)(2,1)} %bitcast.1.og_hbm, bf16[32,2048]{1,0:T(8,128)(2,1)} %bitcast.23, bf16[64,2048]{1,0:T(8,128)(2,1)} %bitcast.4.rw_hbm, s32[8,32]{1,0:T(8,128)} %bitcast.24), custom_call_target="tpu_custom_call" | custom-call | flops 1000000000 | bytes 2000000 | tf_op jit(solution)/shard_map/pack/pallas_call | solution.py:271
  3.0 0.0 copy-start
  3.1 0.0 copy-start.1
  3.1 0.0 copy-start.2
  3.1 63.1 %all_to_all.10.recv_ref = bf16[64,56,256]{2,1,0:T(8,128)(2,1)S(1)} all-to-all(bf16[64,56,256]{2,1,0:T(8,128)(2,1)S(1)} %pack.1), channel_id=1, replica_groups=mesh['section'=16,'expert'=64] {'expert'}, dimensions={0} | all-to-all | bytes 3670016 | tf_op jit(solution)/shard_map/all_to_all | solution.py:356
  66.2 0.0 copy-done
  66.2 0.0 copy-done.1
  66.2 0.0 copy-done.2
  66.2 2.1 %expert.1 = (bf16[384,384]{1,0:T(8,128)(2,1)S(1)}, f32[256,128]{1,0:T(8,128)}) custom-call(bf16[64,56,256]{2,1,0:T(8,128)(2,1)S(1)} %all_to_all.10.recv_ref, bf16[384,2048]{1,0:T(8,128)(2,1)S(1)} %bitcast.18, bf16[384,384]{1,0:T(8,128)(2,1)S(1)} %bitcast.19, bf16[192,192]{1,0:T(8,128)(2,1)S(1)} %copy-done.2), custom_call_target="tpu_custom_call" | custom-call | flops 1200000000 | bytes 4000000 | tf_op jit(solution)/shard_map/expert/pallas_call | solution.py:285
  68.3 6.1 %all-to-all-start.1 = ((f32[64,4,128]{2,1,0:T(4,128)}), f32[64,4,128]{2,1,0:T(4,128)S(1)}, u32[]{:S(2)}, u32[]{:S(2)}) async-start(f32[64,4,128]{2,1,0:T(4,128)} %bitcast.9), calls=%async_computation.1 | async-start | bytes 262144 | tf_op jit(solution)/shard_map/all_to_all | solution.py:356
  74.4 11.8 %collective-permute-start.2 = (bf16[64,2048]{1,0:T(8,128)(2,1)}, bf16[64,2048]{1,0:T(8,128)(2,1)}, u32[]{:S(2)}, u32[]{:S(2)}) collective-permute-start(bf16[64,2048]{1,0:T(8,128)(2,1)} %bitcast.4.rw_hbm), channel_id=1, source_target_pairs={{0,960},{64,0},{128,64},{192,128},{256,192},{320,256},{384,320},{4... | collective-permute-start | bytes 786440 | tf_op jit(solution)/shard_map/ppermute | solution.py:352
  86.2 2.2 %collective-permute-start.1 = (bf16[32,2048]{1,0:T(8,128)(2,1)}, bf16[32,2048]{1,0:T(8,128)(2,1)S(1)}, u32[]{:S(2)}, u32[]{:S(2)}) collective-permute-start(bf16[32,2048]{1,0:T(8,128)(2,1)} %bitcast.1.og_hbm), channel_id=1, source_target_pairs={{0,960},{64,0},{128,64},{192,128},{256,192},{320,256},{384,320},{4... | collective-permute-start | bytes 393224 | tf_op jit(solution)/shard_map/ppermute | solution.py:352
  88.4 0.7 side.1
  89.2 0.0 all-to-all-done.1
  89.2 0.2 logits.1.tie_ref
  89.4 7.4 %collective-permute-start = (bf16[64,32]{1,0:T(8,128)(2,1)S(1)}, bf16[64,32]{1,0:T(8,128)(2,1)S(1)}, u32[]{:S(2)}, u32[]{:S(2)}) collective-permute-start(bf16[64,32]{1,0:T(8,128)(2,1)S(1)} %logits.1.tie_ref), channel_id=1, source_target_pairs={{0,960},{64,0},{128,64},{192,128},{256,192},{320,256},{384,320},{4... | collective-permute-start | bytes 12296 | tf_op jit(solution)/shard_map/ppermute | solution.py:352
  96.8 1.8 %router.1 = f32[32,64]{1,0:T(8,128)} custom-call(f32[256,128]{1,0:T(8,128)S(1)} %bitcast.17, f32[16,64,128]{2,1,0:T(8,128)S(1)} %get-tuple-element.12.code_ref, f32[16,64,128]{2,1,0:T(8,128)S(1)} %get-tuple-element.13.gate_ref, bf16[64,56,256]{2,1,0:T(8,128)(2,1)S(1)} %all_to_all.10.recv_ref, bf16[64,32]{1,0:T(8,128)(2,1)S(1)} %logits.1.tie_ref), custom_call_target="tpu_custom_call" | custom-call | flops 300000000 | bytes 2000000 | tf_op jit(solution)/shard_map/router/pallas_call | solution.py:336
  98.6 0.0 collective-permute-done.1.og_hbm
  98.6 0.0 collective-permute-done.lg_ref
  98.6 0.0 collective-permute-done.2.rw_hbm
  98.6 2.1 %inputs.1 = bf16[32,2048]{1,0:T(8,128)(2,1)} custom-call(bf16[64,32]{1,0:T(8,128)(2,1)S(1)} %collective-permute-done.lg_ref, bf16[32,2048]{1,0:T(8,128)(2,1)S(1)} %collective-permute-done.1.og_hbm, bf16[64,2048]{1,0:T(8,128)(2,1)} %collective-permute-done.2.rw_hbm), custom_call_target="tpu_custom_call" | custom-call | flops 10000000 | bytes 1000000 | tf_op jit(solution)/shard_map/inputs/pallas_call | solution.py:323
Async XLA Ops:
  3.0 63.1 %copy-start = (bf16[1,1,384,2048]{3,2,1,0:T(8,128)(2,1)S(1)}, bf16[1,1,384,2048]{3,2,1,0:T(8,128)(2,1)}, u32[]{:S(2)}) copy-start(bf16[1,1,384,2048]{3,2,1,0:T(8,128)(2,1)} %param.12) | copy-start | bytes 4718596
  3.1 63.1 %copy-start.1 = (bf16[1,1,384,384]{3,2,1,0:T(8,128)(2,1)S(1)}, bf16[1,1,384,384]{3,2,1,0:T(8,128)(2,1)}, u32[]{:S(2)}) copy-start(bf16[1,1,384,384]{3,2,1,0:T(8,128)(2,1)} %param.11) | copy-start | bytes 884740
  3.1 63.1 %copy-start.2 = (bf16[192,192]{1,0:T(8,128)(2,1)S(1)}, bf16[192,192]{1,0:T(8,128)(2,1)}, u32[]{:S(2)}) copy-start(bf16[192,192]{1,0:T(8,128)(2,1)} %constant.6.clone.perm_ref) | copy-start | bytes 221188
  68.3 20.9 %all-to-all-start.1 = ((f32[64,4,128]{2,1,0:T(4,128)}), f32[64,4,128]{2,1,0:T(4,128)S(1)}, u32[]{:S(2)}, u32[]{:S(2)}) async-start(f32[64,4,128]{2,1,0:T(4,128)} %bitcast.9), calls=%async_computation.1 | async-start | bytes 262144 | tf_op jit(solution)/shard_map/all_to_all | solution.py:356
  74.4 24.2 %collective-permute-start.2 = (bf16[64,2048]{1,0:T(8,128)(2,1)}, bf16[64,2048]{1,0:T(8,128)(2,1)}, u32[]{:S(2)}, u32[]{:S(2)}) collective-permute-start(bf16[64,2048]{1,0:T(8,128)(2,1)} %bitcast.4.rw_hbm), channel_id=1, source_target_pairs={{0,960},{64,0},{128,64},{192,128},{256,192},{320,256},{384,320},{4... | collective-permute-start | bytes 786440 | tf_op jit(solution)/shard_map/ppermute | solution.py:352
  86.2 12.4 %collective-permute-start.1 = (bf16[32,2048]{1,0:T(8,128)(2,1)}, bf16[32,2048]{1,0:T(8,128)(2,1)S(1)}, u32[]{:S(2)}, u32[]{:S(2)}) collective-permute-start(bf16[32,2048]{1,0:T(8,128)(2,1)} %bitcast.1.og_hbm), channel_id=1, source_target_pairs={{0,960},{64,0},{128,64},{192,128},{256,192},{320,256},{384,320},{4... | collective-permute-start | bytes 393224 | tf_op jit(solution)/shard_map/ppermute | solution.py:352
  89.4 9.2 %collective-permute-start = (bf16[64,32]{1,0:T(8,128)(2,1)S(1)}, bf16[64,32]{1,0:T(8,128)(2,1)S(1)}, u32[]{:S(2)}, u32[]{:S(2)}) collective-permute-start(bf16[64,32]{1,0:T(8,128)(2,1)S(1)} %logits.1.tie_ref), channel_id=1, source_target_pairs={{0,960},{64,0},{128,64},{192,128},{256,192},{320,256},{384,320},{4... | collective-permute-start | bytes 12296 | tf_op jit(solution)/shard_map/ppermute | solution.py:352

commit v5 on v4

--- a/solution.py
+++ b/solution.py
@@ -169,8 +169,8 @@
             named = jnp.where(hit, 1.0, named)
             dense = jnp.where(hit, gates[k : k + 1, :], dense)
         rank = dot(named.astype(BF16), ahead, 1, 0)
-        code_ref[g] = jnp.where(named > 0.5, rank, -1.0)
-        gate_ref[g] = dense
+        code_ref[g] = jnp.where(named > 0.5, rank, -1.0).astype(BF16)
+        gate_ref[g] = dense.astype(BF16)
     copy.wait()
 
 
@@ -180,8 +180,8 @@
     offset = ((me // 4) % 4) * 32 + (me % 4) * CAP
     mine = pltpu.roll(mine, (128 - offset) % 128, axis=1)
     back = (128 - (me % 4) * TOK) % 128
-    code = pltpu.roll(code_ref[me // 4], back, axis=1)[:, :TOK]
-    gate = pltpu.roll(gate_ref[me // 4], back, axis=1)[:, :TOK]
+    code = pltpu.roll(code_ref[me // 4].astype(F32), back, axis=1)[:, :TOK]
+    gate = pltpu.roll(gate_ref[me // 4].astype(F32), back, axis=1)[:, :TOK]
     sdg = jnp.zeros((PEERS, TOK), F32)
     for c in range(CAP):
         sdg = jnp.where(code == c, mine[:, c : c + 1], sdg)
@@ -189,27 +189,16 @@
     out_ref[...] = (sdg - gate * total).astype(BF16)
 
 
-def input_kernel(lg_ref, og_hbm, rw_hbm, out_hbm, og_ref, rw_ref, out_ref, sems):
-    spans = [pl.ds(i * 512, 512) for i in range(4)]
-    loads = [
-        pltpu.make_async_copy(rw_hbm.at[:, at], rw_ref.at[:, at], sems.at[i])
-        for i, at in enumerate(spans)
-    ] + [pltpu.make_async_copy(og_hbm, og_ref, sems.at[8])]
-    stores = [
-        pltpu.make_async_copy(out_ref.at[:, at], out_hbm.at[:, at], sems.at[4 + i])
-        for i, at in enumerate(spans)
-    ]
-    for copy in loads:
-        copy.start()
+def input_kernel(lg_ref, og_ref, rw_ref, out_hbm, out_ref, sems):
     lg = lg_ref[...]
-    for i, at in enumerate(spans):
-        loads[i].wait()
+    copies = []
+    for i in range(2):
+        at = pl.ds(i * 1024, 1024)
         part = dot(lg, rw_ref[:, at], 0, 0)
-        if i == 0:
-            loads[4].wait()
         out_ref[:, at] = (og_ref[:, at].astype(F32) + part).astype(BF16)
-        stores[i].start()
-    for copy in stores:
+        copies.append(pltpu.make_async_copy(out_ref.at[:, at], out_hbm.at[:, at], sems.at[i]))
+        copies[i].start()
+    for copy in copies:
         copy.wait()
 
 
@@ -235,12 +224,12 @@
             low = (rest - mid).astype(BF16).astype(F32)
             z = hi + pltpu.roll(mid, 32, axis=1) + pltpu.roll(low, 64, axis=1)
             wide = dot(z.astype(BF16), spread_ref[...], 1, 0)
-            code = code_ref[g]
+            code = code_ref[g].astype(F32)
             sdg = jnp.zeros((PEERS, 128), F32)
             for c in range(CAP):
                 sdg = jnp.where(code == c, wide[:, c * 128 : (c + 1) * 128], sdg)
             total = jnp.sum(sdg, axis=0, keepdims=True)
-            lg_ref[:, g * 128 : (g + 1) * 128] = (sdg - gate_ref[g] * total).astype(BF16)
+            lg_ref[:, g * 128 : (g + 1) * 128] = (sdg - gate_ref[g].astype(F32) * total).astype(BF16)
     out_ref[...] = dot(cols_ref[...].astype(BF16), lg_ref[...], 1, 1)
 
 
@@ -296,8 +285,8 @@
     return call(
         side_kernel,
         (
-            struct((GROUPS, PEERS, 128), F32),
-            struct((GROUPS, PEERS, 128), F32),
+            struct((GROUPS, PEERS, 128), BF16),
+            struct((GROUPS, PEERS, 128), BF16),
             struct(hg.shape, BF16),
         ),
         [pltpu.SemaphoreType.DMA],
@@ -323,10 +312,9 @@
     return call(
         input_kernel,
         struct(og.shape, BF16),
-        [pltpu.VMEM(a.shape, BF16) for a in (og, rw, og)] + [pltpu.SemaphoreType.DMA((9,))],
+        [pltpu.VMEM(og.shape, BF16), pltpu.SemaphoreType.DMA((2,))],
         flops=10**7,
         moved=10**6,
-        in_specs=[whole(), far(), far()],
         out_specs=far(),
         name="inputs",
     )(lg, og, rw)

time: 101 us -> 99.8 us (0.988)
  Pallas kernels: 9.43 us -> 8.21 us
    pallas_call x2, Pallas kernels: 2.85 us -> 1.61 us  [the longest x1 0.87 us: input_grads(): call(input_kernel, struct(og.shape, BF16), [pltpu.VMEM(og.shape, BF16), p...]
where the time goes in v5:
time: 99.8 us; the launch traced here: 99.5 us
  blocking collectives  63.1 us (63%)
  starting transfers between devices  27.5 us (28%)
  Pallas kernels  8.21 us (8%)
    all_to_all x1, blocking collectives, exchange(): return lax.all_to_all(x, 'expert', split_axis=0, concat_axis=0, tiled=True)  63.1 us
    ppermute x3, starting transfers between devices, shifted(): return lax.ppermute(x, 'section', [(i, (i - 1) % n) for i in range(n)])  21.4 us
    all_to_all x1, starting transfers between devices, exchange(): return lax.all_to_all(x, 'expert', split_axis=0, concat_axis=0, tiled=True)  6.09 us
    pallas_call x1, Pallas kernels, pack(): call(pack_kernel, struct((PEERS, CHUNK, WIDE), BF16), [pltpu.VMEM(a.shape...  2.41 us
    pallas_call x1, Pallas kernels, expert(): call(expert_kernel, (struct((SLOTS, SLOTS), BF16), struct((PEERS * 4, 128...  2.15 us
  transfers between devices with their start and end apart: 4, of which 0 were waited for; matrix products, arithmetic and copies ran while one was open for 0% of the time, Pallas kernels for 3%

profile of v5, /device:TPU:1, one launch (start us, length us, event | category | flops | bytes accessed | tf_op | source)
XLA Modules:
  0.0 99.5 jit_solution(10846683814518074038)
XLA Ops:
  0.6 2.4 %pack.1 = bf16[64,56,256]{2,1,0:T(8,128)(2,1)S(1)} custom-call(bf16[32,2048]{1,0:T(8,128)(2,1)} %bitcast.1.og_hbm, bf16[32,2048]{1,0:T(8,128)(2,1)} %bitcast.25, bf16[64,2048]{1,0:T(8,128)(2,1)} %bitcast.23, s32[8,32]{1,0:T(8,128)} %bitcast.26), custom_call_target="tpu_custom_call" | custom-call | flops 1000000000 | bytes 2000000 | tf_op jit(solution)/shard_map/pack/pallas_call | solution.py:260
  3.0 0.0 copy-start
  3.1 0.0 copy-start.1
  3.1 0.0 copy-start.2
  3.1 63.1 %all_to_all.10.recv_ref = bf16[64,56,256]{2,1,0:T(8,128)(2,1)S(1)} all-to-all(bf16[64,56,256]{2,1,0:T(8,128)(2,1)S(1)} %pack.1), channel_id=1, replica_groups=mesh['section'=16,'expert'=64] {'expert'}, dimensions={0} | all-to-all | bytes 3670016 | tf_op jit(solution)/shard_map/all_to_all | solution.py:344
  66.2 0.0 copy-done
  66.2 0.0 copy-done.1
  66.2 0.0 copy-done.2
  66.2 0.0 copy-start.3
  66.2 2.2 %expert.1 = (bf16[384,384]{1,0:T(8,128)(2,1)S(1)}, f32[256,128]{1,0:T(8,128)}) custom-call(bf16[64,56,256]{2,1,0:T(8,128)(2,1)S(1)} %all_to_all.10.recv_ref, bf16[384,2048]{1,0:T(8,128)(2,1)S(1)} %bitcast.18, bf16[384,384]{1,0:T(8,128)(2,1)S(1)} %bitcast.19, bf16[192,192]{1,0:T(8,128)(2,1)S(1)} %copy-done.2), custom_call_target="tpu_custom_call" | custom-call | flops 1200000000 | bytes 4000000 | tf_op jit(solution)/shard_map/expert/pallas_call | solution.py:274
  68.3 6.1 %all-to-all-start.1 = ((f32[64,4,128]{2,1,0:T(4,128)}), f32[64,4,128]{2,1,0:T(4,128)S(1)}, u32[]{:S(2)}, u32[]{:S(2)}) async-start(f32[64,4,128]{2,1,0:T(4,128)} %bitcast.9), calls=%async_computation.1 | async-start | bytes 262144 | tf_op jit(solution)/shard_map/all_to_all | solution.py:344
  74.4 0.0 copy-done.3
  74.4 11.8 %collective-permute-start.2 = (bf16[64,2048]{1,0:T(8,128)(2,1)S(1)}, bf16[64,2048]{1,0:T(8,128)(2,1)S(1)}, u32[]{:S(2)}, u32[]{:S(2)}) collective-permute-start(bf16[64,2048]{1,0:T(8,128)(2,1)S(1)} %bitcast.24), channel_id=1, source_target_pairs={{0,960},{64,0},{128,64},{192,128},{256,192},{320,256},{384,320},{4... | collective-permute-start | bytes 786440 | tf_op jit(solution)/shard_map/ppermute | solution.py:340
  86.3 2.2 %collective-permute-start.1 = (bf16[32,2048]{1,0:T(8,128)(2,1)}, bf16[32,2048]{1,0:T(8,128)(2,1)S(1)}, u32[]{:S(2)}, u32[]{:S(2)}) collective-permute-start(bf16[32,2048]{1,0:T(8,128)(2,1)} %bitcast.1.og_hbm), channel_id=1, source_target_pairs={{0,960},{64,0},{128,64},{192,128},{256,192},{320,256},{384,320},{4... | collective-permute-start | bytes 393224 | tf_op jit(solution)/shard_map/ppermute | solution.py:340
  88.5 0.7 side.1
  89.2 0.0 all-to-all-done.1
  89.2 0.2 logits.1.tie_ref
  89.5 7.4 %collective-permute-start = (bf16[64,32]{1,0:T(8,128)(2,1)S(1)}, bf16[64,32]{1,0:T(8,128)(2,1)S(1)}, u32[]{:S(2)}, u32[]{:S(2)}) collective-permute-start(bf16[64,32]{1,0:T(8,128)(2,1)S(1)} %logits.1.tie_ref), channel_id=1, source_target_pairs={{0,960},{64,0},{128,64},{192,128},{256,192},{320,256},{384,320},{4... | collective-permute-start | bytes 12296 | tf_op jit(solution)/shard_map/ppermute | solution.py:340
  96.8 1.8 %router.1 = f32[32,64]{1,0:T(8,128)} custom-call(f32[256,128]{1,0:T(8,128)S(1)} %bitcast.17, bf16[16,64,128]{2,1,0:T(8,128)(2,1)S(1)} %get-tuple-element.12.code_ref, bf16[16,64,128]{2,1,0:T(8,128)(2,1)S(1)} %get-tuple-element.13.gate_ref, bf16[64,56,256]{2,1,0:T(8,128)(2,1)S(1)} %all_to_all.10.recv_ref, bf16[64,32]{1,0:T(8,128)(2,1)S(1)} %logits.1.tie_ref), custom_call_target="tpu_custom_call" | custom-call | flops 300000000 | bytes 2000000 | tf_op jit(solution)/shard_map/router/pallas_call | solution.py:324
  98.7 0.0 collective-permute-done.1.og_ref
  98.7 0.0 collective-permute-done.lg_ref
  98.7 0.0 collective-permute-done.2.rw_ref
  98.7 0.9 inputs.1
Async XLA Ops:
  3.0 63.1 %copy-start = (bf16[1,1,384,2048]{3,2,1,0:T(8,128)(2,1)S(1)}, bf16[1,1,384,2048]{3,2,1,0:T(8,128)(2,1)}, u32[]{:S(2)}) copy-start(bf16[1,1,384,2048]{3,2,1,0:T(8,128)(2,1)} %param.12) | copy-start | bytes 4718596
  3.1 63.1 %copy-start.1 = (bf16[1,1,384,384]{3,2,1,0:T(8,128)(2,1)S(1)}, bf16[1,1,384,384]{3,2,1,0:T(8,128)(2,1)}, u32[]{:S(2)}) copy-start(bf16[1,1,384,384]{3,2,1,0:T(8,128)(2,1)} %param.11) | copy-start | bytes 884740
  3.1 63.1 %copy-start.2 = (bf16[192,192]{1,0:T(8,128)(2,1)S(1)}, bf16[192,192]{1,0:T(8,128)(2,1)}, u32[]{:S(2)}) copy-start(bf16[192,192]{1,0:T(8,128)(2,1)} %constant.6.clone.perm_ref) | copy-start | bytes 221188
  66.2 8.3 %copy-start.3 = (bf16[1,2048,64]{1,2,0:T(8,128)(2,1)S(1)}, bf16[1,2048,64]{1,2,0:T(8,128)(2,1)}, u32[]{:S(2)}) copy-start(bf16[1,2048,64]{1,2,0:T(8,128)(2,1)} %param.9) | copy-start | bytes 786436
  68.3 20.9 %all-to-all-start.1 = ((f32[64,4,128]{2,1,0:T(4,128)}), f32[64,4,128]{2,1,0:T(4,128)S(1)}, u32[]{:S(2)}, u32[]{:S(2)}) async-start(f32[64,4,128]{2,1,0:T(4,128)} %bitcast.9), calls=%async_computation.1 | async-start | bytes 262144 | tf_op jit(solution)/shard_map/all_to_all | solution.py:344
  74.4 24.2 %collective-permute-start.2 = (bf16[64,2048]{1,0:T(8,128)(2,1)S(1)}, bf16[64,2048]{1,0:T(8,128)(2,1)S(1)}, u32[]{:S(2)}, u32[]{:S(2)}) collective-permute-start(bf16[64,2048]{1,0:T(8,128)(2,1)S(1)} %bitcast.24), channel_id=1, source_target_pairs={{0,960},{64,0},{128,64},{192,128},{256,192},{320,256},{384,320},{4... | collective-permute-start | bytes 786440 | tf_op jit(solution)/shard_map/ppermute | solution.py:340
  86.3 12.4 %collective-permute-start.1 = (bf16[32,2048]{1,0:T(8,128)(2,1)}, bf16[32,2048]{1,0:T(8,128)(2,1)S(1)}, u32[]{:S(2)}, u32[]{:S(2)}) collective-permute-start(bf16[32,2048]{1,0:T(8,128)(2,1)} %bitcast.1.og_hbm), channel_id=1, source_target_pairs={{0,960},{64,0},{128,64},{192,128},{256,192},{320,256},{384,320},{4... | collective-permute-start | bytes 393224 | tf_op jit(solution)/shard_map/ppermute | solution.py:340
  89.5 9.2 %collective-permute-start = (bf16[64,32]{1,0:T(8,128)(2,1)S(1)}, bf16[64,32]{1,0:T(8,128)(2,1)S(1)}, u32[]{:S(2)}, u32[]{:S(2)}) collective-permute-start(bf16[64,32]{1,0:T(8,128)(2,1)S(1)} %logits.1.tie_ref), channel_id=1, source_target_pairs={{0,960},{64,0},{128,64},{192,128},{256,192},{320,256},{384,320},{4... | collective-permute-start | bytes 12296 | tf_op jit(solution)/shard_map/ppermute | solution.py:340

commit v6 on v5

--- a/solution.py
+++ b/solution.py
@@ -130,17 +130,13 @@
     hg_ref[...] = grad.astype(BF16)
     prod = grad * h_ref[...].astype(F32)
     part = prod[:, :128] + prod[:, 128:256] + prod[:, 256:]
-    gap = jnp.zeros((8, 128), F32)
-    pieces = []
-    for g in range(GROUPS):
-        pieces += [part[g * 24 : (g + 1) * 24], gap]
-    padded = jnp.concatenate(pieces, axis=0)
-    line = jnp.sum(padded.T, axis=0, keepdims=True)
-    which = iota((8, 128), 0) & 3
-    out = jnp.zeros((8, 128), F32)
-    for t in range(4):
+    line = jnp.sum(part.T, axis=0, keepdims=True)
+    row = iota((24, 128), 0)
+    which = row - 3 * ((row.astype(F32) + 0.5) * (1 / 3)).astype(jnp.int32)
+    out = jnp.zeros((24, 128), F32)
+    for t in range(3):
         out = jnp.where(which == t, line[:, t * 128 : (t + 1) * 128], out)
-    sdg_ref[...] = jnp.broadcast_to(out[None], (PEERS // 2, 8, 128)).reshape(PEERS * 4, 128)
+    sdg_ref[...] = jnp.broadcast_to(out[None], (8, 24, 128)).reshape(PEERS * 3, 128)
 
 
 def gather(blocks, at):
@@ -176,9 +172,12 @@
 
 def logit_kernel(me_ref, s_ref, code_ref, gate_ref, out_ref):
     me = me_ref[0]
-    mine = s_ref[pl.ds(me // 16, PEERS, stride=4), :]
-    offset = ((me // 4) % 4) * 32 + (me % 4) * CAP
-    mine = pltpu.roll(mine, (128 - offset) % 128, axis=1)
+    tile, offset = me * CAP // 128, me * CAP % 128
+    mine, after = [
+        pltpu.roll(s_ref[pl.ds(t, PEERS, stride=3), :], (128 - offset) % 128, axis=1)
+        for t in (tile, jnp.minimum(tile + 1, 2))
+    ]
+    mine = jnp.where(iota((PEERS, 128), 1) < 128 - offset, mine, after)
     back = (128 - (me % 4) * TOK) % 128
     code = pltpu.roll(code_ref[me // 4].astype(F32), back, axis=1)[:, :TOK]
     gate = pltpu.roll(gate_ref[me // 4].astype(F32), back, axis=1)[:, :TOK]
@@ -212,24 +211,25 @@
         for h in range(4):
             cols_ref[h * 8 : (h + 1) * 8, g * 128 : (g + 1) * 128] = gather(cols, h)
     lane = iota((PEERS, 128), 1)
-    for t in range(4):
-        tile = s_ref[pl.ds(t, PEERS, stride=4), :]
-        for q in range(4):
-            g = t * 4 + q
-            x = pltpu.roll(tile, 128 - 32 * q, axis=1) if q else tile
-            x = jnp.where(lane < 24, x, 0.0)
-            hi = x.astype(BF16).astype(F32)
-            rest = x - hi
-            mid = rest.astype(BF16).astype(F32)
-            low = (rest - mid).astype(BF16).astype(F32)
-            z = hi + pltpu.roll(mid, 32, axis=1) + pltpu.roll(low, 64, axis=1)
-            wide = dot(z.astype(BF16), spread_ref[...], 1, 0)
-            code = code_ref[g].astype(F32)
-            sdg = jnp.zeros((PEERS, 128), F32)
-            for c in range(CAP):
-                sdg = jnp.where(code == c, wide[:, c * 128 : (c + 1) * 128], sdg)
-            total = jnp.sum(sdg, axis=0, keepdims=True)
-            lg_ref[:, g * 128 : (g + 1) * 128] = (sdg - gate_ref[g].astype(F32) * total).astype(BF16)
+    tiles = [s_ref[pl.ds(t, PEERS, stride=3), :] for t in range(3)]
+    for g in range(GROUPS):
+        t, offset = g * 24 // 128, g * 24 % 128
+        x = pltpu.roll(tiles[t], 128 - offset, axis=1) if offset else tiles[t]
+        if offset + 24 > 128:
+            x = jnp.where(lane < 128 - offset, x, pltpu.roll(tiles[t + 1], 128 - offset, axis=1))
+        x = jnp.where(lane < 24, x, 0.0)
+        hi = x.astype(BF16).astype(F32)
+        rest = x - hi
+        mid = rest.astype(BF16).astype(F32)
+        low = (rest - mid).astype(BF16).astype(F32)
+        z = hi + pltpu.roll(mid, 32, axis=1) + pltpu.roll(low, 64, axis=1)
+        wide = dot(z.astype(BF16), spread_ref[...], 1, 0)
+        code = code_ref[g].astype(F32)
+        sdg = jnp.zeros((PEERS, 128), F32)
+        for c in range(CAP):
+            sdg = jnp.where(code == c, wide[:, c * 128 : (c + 1) * 128], sdg)
+        total = jnp.sum(sdg, axis=0, keepdims=True)
+        lg_ref[:, g * 128 : (g + 1) * 128] = (sdg - gate_ref[g].astype(F32) * total).astype(BF16)
     out_ref[...] = dot(cols_ref[...].astype(BF16), lg_ref[...], 1, 1)
 
 
@@ -273,7 +273,7 @@
 def expert(recv, w, h, perm):
     return call(
         expert_kernel,
-        (struct((SLOTS, SLOTS), BF16), struct((PEERS * 4, 128), F32)),
+        (struct((SLOTS, SLOTS), BF16), struct((PEERS * 3, 128), F32)),
         [pltpu.VMEM((SLOTS, PARTS * WIDE), BF16)],
         flops=12 * 10**8,
         moved=4 * 10**6,
@@ -329,7 +329,7 @@
             pltpu.VMEM((128, CAP * 128), BF16),
             pltpu.VMEM((PEERS, PEERS * TOK), BF16),
         ],
-        flops=3 * 10**8,
+        flops=10**9,
         moved=2 * 10**6,
         name="router",
     )(s, code, gate, recv, tie)
@@ -355,7 +355,7 @@
     hidden_near, sdg = expert(
         recv, down_weight[0, 0], hidden_act[0, 0], jnp.asarray(compaction(), BF16)
     )
-    back = exchange(sdg.reshape(PEERS, 4, 128)).reshape(PEERS * 4, 128)
+    back = exchange(sdg.reshape(PEERS, 1, SLOTS)).reshape(PEERS * 3, 128)
     og_held, rw_held, sdg = lax.optimization_barrier((og, rw, sdg))
     og_next, rw_next = shifted(og_held), shifted(rw_held)
     all_gate, all_code, hidden_grad = side(recv, hidden_near)

time: 99.8 us -> 99.7 us (level)
  no operation moved by 1% of the time
where the time goes in v6:
time: 99.7 us; the launch traced here: 99.4 us
  blocking collectives  63.1 us (63%)
  starting transfers between devices  27.3 us (27%)
  Pallas kernels  8.21 us (8%)
    all_to_all x1, blocking collectives, exchange(): return lax.all_to_all(x, 'expert', split_axis=0, concat_axis=0, tiled=True)  63.1 us
    ppermute x3, starting transfers between devices, shifted(): return lax.ppermute(x, 'section', [(i, (i - 1) % n) for i in range(n)])  21.2 us
    all_to_all x1, starting transfers between devices, exchange(): return lax.all_to_all(x, 'expert', split_axis=0, concat_axis=0, tiled=True)  6.09 us
    pallas_call x1, Pallas kernels, pack(): call(pack_kernel, struct((PEERS, CHUNK, WIDE), BF16), [pltpu.VMEM(a.shape...  2.41 us
    pallas_call x1, Pallas kernels, expert(): call(expert_kernel, (struct((SLOTS, SLOTS), BF16), struct((PEERS * 3, 128...  2.12 us
  transfers between devices with their start and end apart: 4, of which 0 were waited for; matrix products, arithmetic and copies ran while one was open for 0% of the time, Pallas kernels for 3%

profile of v6, /device:TPU:1, one launch (start us, length us, event | category | flops | bytes accessed | tf_op | source)
XLA Modules:
  0.0 99.4 jit_solution(17009857101570098203)
XLA Ops:
  0.6 2.4 %pack.1 = bf16[64,56,256]{2,1,0:T(8,128)(2,1)S(1)} custom-call(bf16[32,2048]{1,0:T(8,128)(2,1)} %bitcast.25, bf16[32,2048]{1,0:T(8,128)(2,1)} %bitcast.24, bf16[64,2048]{1,0:T(8,128)(2,1)} %bitcast.22, s32[8,32]{1,0:T(8,128)} %bitcast.27), custom_call_target="tpu_custom_call" | custom-call | flops 1000000000 | bytes 2000000 | tf_op jit(solution)/shard_map/pack/pallas_call | solution.py:260
  3.0 0.0 copy-start
  3.1 0.0 copy-start.1
  3.1 0.0 copy-start.2
  3.1 63.1 %all_to_all.10.recv_ref = bf16[64,56,256]{2,1,0:T(8,128)(2,1)S(1)} all-to-all(bf16[64,56,256]{2,1,0:T(8,128)(2,1)S(1)} %pack.1), channel_id=1, replica_groups=mesh['section'=16,'expert'=64] {'expert'}, dimensions={0} | all-to-all | bytes 3670016 | tf_op jit(solution)/shard_map/all_to_all | solution.py:344
  66.2 0.0 copy-done
  66.2 0.0 copy-done.1
  66.2 0.0 copy-done.2
  66.2 0.0 copy-start.3
  66.2 0.0 copy-start.4
  66.2 2.1 %expert.1 = (bf16[384,384]{1,0:T(8,128)(2,1)S(1)}, f32[192,128]{1,0:T(8,128)}) custom-call(bf16[64,56,256]{2,1,0:T(8,128)(2,1)S(1)} %all_to_all.10.recv_ref, bf16[384,2048]{1,0:T(8,128)(2,1)S(1)} %bitcast.18, bf16[384,384]{1,0:T(8,128)(2,1)S(1)} %bitcast.19, bf16[192,192]{1,0:T(8,128)(2,1)S(1)} %copy-done.2), custom_call_target="tpu_custom_call" | custom-call | flops 1200000000 | bytes 4000000 | tf_op jit(solution)/shard_map/expert/pallas_call | solution.py:274
  68.3 6.1 %all-to-all-start.1 = ((f32[64,1,384]{2,1,0:T(1,128)}), f32[64,1,384]{2,1,0:T(1,128)S(1)}, u32[]{:S(2)}, u32[]{:S(2)}) async-start(f32[64,1,384]{2,1,0:T(1,128)} %bitcast.9), calls=%async_computation.1 | async-start | bytes 196608 | tf_op jit(solution)/shard_map/all_to_all | solution.py:344
  74.4 0.0 copy-done.3
  74.4 11.8 %collective-permute-start.2 = (bf16[64,2048]{1,0:T(8,128)(2,1)S(1)}, bf16[64,2048]{1,0:T(8,128)(2,1)S(1)}, u32[]{:S(2)}, u32[]{:S(2)}) collective-permute-start(bf16[64,2048]{1,0:T(8,128)(2,1)S(1)} %bitcast.23), channel_id=1, source_target_pairs={{0,960},{64,0},{128,64},{192,128},{256,192},{320,256},{384,320},{4... | collective-permute-start | bytes 786440 | tf_op jit(solution)/shard_map/ppermute | solution.py:340
  86.3 0.0 copy-done.4
  86.3 2.2 %collective-permute-start.1 = (bf16[32,2048]{1,0:T(8,128)(2,1)S(1)}, bf16[32,2048]{1,0:T(8,128)(2,1)S(1)}, u32[]{:S(2)}, u32[]{:S(2)}) collective-permute-start(bf16[32,2048]{1,0:T(8,128)(2,1)S(1)} %bitcast.26), channel_id=1, source_target_pairs={{0,960},{64,0},{128,64},{192,128},{256,192},{320,256},{384,320},{4... | collective-permute-start | bytes 393224 | tf_op jit(solution)/shard_map/ppermute | solution.py:340
  88.5 0.7 side.1
  89.2 0.0 all-to-all-done.1
  89.2 0.2 logits.1.tie_ref
  89.5 7.2 %collective-permute-start = (bf16[64,32]{1,0:T(8,128)(2,1)S(1)}, bf16[64,32]{1,0:T(8,128)(2,1)S(1)}, u32[]{:S(2)}, u32[]{:S(2)}) collective-permute-start(bf16[64,32]{1,0:T(8,128)(2,1)S(1)} %logits.1.tie_ref), channel_id=1, source_target_pairs={{0,960},{64,0},{128,64},{192,128},{256,192},{320,256},{384,320},{4... | collective-permute-start | bytes 12296 | tf_op jit(solution)/shard_map/ppermute | solution.py:340
  96.7 1.8 %router.1 = f32[32,64]{1,0:T(8,128)} custom-call(f32[192,128]{1,0:T(8,128)S(1)} %bitcast.17, bf16[16,64,128]{2,1,0:T(8,128)(2,1)S(1)} %get-tuple-element.12.code_ref, bf16[16,64,128]{2,1,0:T(8,128)(2,1)S(1)} %get-tuple-element.13.gate_ref, bf16[64,56,256]{2,1,0:T(8,128)(2,1)S(1)} %all_to_all.10.recv_ref, bf16[64,32]{1,0:T(8,128)(2,1)S(1)} %logits.1.tie_ref), custom_call_target="tpu_custom_call" | custom-call | flops 1000000000 | bytes 2000000 | tf_op jit(solution)/shard_map/router/pallas_call | solution.py:324
  98.5 0.0 collective-permute-done.1.og_ref
  98.5 0.0 collective-permute-done.lg_ref
  98.5 0.0 collective-permute-done.2.rw_ref
  98.5 0.9 inputs.1
Async XLA Ops:
  3.0 63.1 %copy-start = (bf16[1,1,384,2048]{3,2,1,0:T(8,128)(2,1)S(1)}, bf16[1,1,384,2048]{3,2,1,0:T(8,128)(2,1)}, u32[]{:S(2)}) copy-start(bf16[1,1,384,2048]{3,2,1,0:T(8,128)(2,1)} %param.12) | copy-start | bytes 4718596
  3.1 63.1 %copy-start.1 = (bf16[1,1,384,384]{3,2,1,0:T(8,128)(2,1)S(1)}, bf16[1,1,384,384]{3,2,1,0:T(8,128)(2,1)}, u32[]{:S(2)}) copy-start(bf16[1,1,384,384]{3,2,1,0:T(8,128)(2,1)} %param.11) | copy-start | bytes 884740
  3.1 63.1 %copy-start.2 = (bf16[192,192]{1,0:T(8,128)(2,1)S(1)}, bf16[192,192]{1,0:T(8,128)(2,1)}, u32[]{:S(2)}) copy-start(bf16[192,192]{1,0:T(8,128)(2,1)} %constant.6.clone.perm_ref) | copy-start | bytes 221188
  66.2 8.2 %copy-start.3 = (bf16[1,2048,64]{1,2,0:T(8,128)(2,1)S(1)}, bf16[1,2048,64]{1,2,0:T(8,128)(2,1)}, u32[]{:S(2)}) copy-start(bf16[1,2048,64]{1,2,0:T(8,128)(2,1)} %param.9) | copy-start | bytes 786436
  66.2 20.1 %copy-start.4 = (bf16[1,32,2048]{2,1,0:T(8,128)(2,1)S(1)}, bf16[1,32,2048]{2,1,0:T(8,128)(2,1)}, u32[]{:S(2)}) copy-start(bf16[1,32,2048]{2,1,0:T(8,128)(2,1)} %param.7) | copy-start | bytes 393220
  68.3 20.9 %all-to-all-start.1 = ((f32[64,1,384]{2,1,0:T(1,128)}), f32[64,1,384]{2,1,0:T(1,128)S(1)}, u32[]{:S(2)}, u32[]{:S(2)}) async-start(f32[64,1,384]{2,1,0:T(1,128)} %bitcast.9), calls=%async_computation.1 | async-start | bytes 196608 | tf_op jit(solution)/shard_map/all_to_all | solution.py:344
  74.4 24.1 %collective-permute-start.2 = (bf16[64,2048]{1,0:T(8,128)(2,1)S(1)}, bf16[64,2048]{1,0:T(8,128)(2,1)S(1)}, u32[]{:S(2)}, u32[]{:S(2)}) collective-permute-start(bf16[64,2048]{1,0:T(8,128)(2,1)S(1)} %bitcast.23), channel_id=1, source_target_pairs={{0,960},{64,0},{128,64},{192,128},{256,192},{320,256},{384,320},{4... | collective-permute-start | bytes 786440 | tf_op jit(solution)/shard_map/ppermute | solution.py:340
  86.3 12.2 %collective-permute-start.1 = (bf16[32,2048]{1,0:T(8,128)(2,1)S(1)}, bf16[32,2048]{1,0:T(8,128)(2,1)S(1)}, u32[]{:S(2)}, u32[]{:S(2)}) collective-permute-start(bf16[32,2048]{1,0:T(8,128)(2,1)S(1)} %bitcast.26), channel_id=1, source_target_pairs={{0,960},{64,0},{128,64},{192,128},{256,192},{320,256},{384,320},{4... | collective-permute-start | bytes 393224 | tf_op jit(solution)/shard_map/ppermute | solution.py:340
  89.5 9.0 %collective-permute-start = (bf16[64,32]{1,0:T(8,128)(2,1)S(1)}, bf16[64,32]{1,0:T(8,128)(2,1)S(1)}, u32[]{:S(2)}, u32[]{:S(2)}) collective-permute-start(bf16[64,32]{1,0:T(8,128)(2,1)S(1)} %logits.1.tie_ref), channel_id=1, source_target_pairs={{0,960},{64,0},{128,64},{192,128},{256,192},{320,256},{384,320},{4... | collective-permute-start | bytes 12296 | tf_op jit(solution)/shard_map/ppermute | solution.py:340

commit v7 on v6

--- a/solution.py
+++ b/solution.py
@@ -43,11 +43,18 @@
 
 
 def pack_kernel(
-    og_hbm, li_hbm, rw_hbm, ids_hbm, send_ref, og_ref, li_ref, rw_ref, ids_ref, gt_ref, ct_ref, sems
+    og_hbm, li_hbm, rw_hbm, ids_hbm, send_ref, near_hbm,
+    og_ref, li_ref, rw_ref, ids_ref, gt_ref, ct_ref, sems,
 ):
     pairs = ((ids_hbm, ids_ref), (rw_hbm, rw_ref), (li_hbm, li_ref), (og_hbm, og_ref))
     copies = [pltpu.make_async_copy(a, b, sems.at[i]) for i, (a, b) in enumerate(pairs)]
     for copy in copies:
+        copy.start()
+    joins = [
+        pltpu.make_async_copy(og_hbm, near_hbm.at[pl.ds(0, TOK)], sems.at[4]),
+        pltpu.make_async_copy(rw_hbm, near_hbm.at[pl.ds(TOK, PEERS)], sems.at[5]),
+    ]
+    for copy in joins:
         copy.start()
     copies[0].wait()
     ids = ids_ref[...]
@@ -113,6 +120,8 @@
         return carry
 
     lax.fori_loop(0, PEERS // 8, step, 0, unroll=8)
+    for copy in joins:
+        copy.wait()
 
 
 def expert_kernel(recv_ref, w_ref, h_ref, perm_ref, hg_ref, sdg_ref, rows_ref):
@@ -188,13 +197,13 @@
     out_ref[...] = (sdg - gate * total).astype(BF16)
 
 
-def input_kernel(lg_ref, og_ref, rw_ref, out_hbm, out_ref, sems):
+def input_kernel(lg_ref, near_ref, out_hbm, out_ref, sems):
     lg = lg_ref[...]
     copies = []
     for i in range(2):
         at = pl.ds(i * 1024, 1024)
-        part = dot(lg, rw_ref[:, at], 0, 0)
-        out_ref[:, at] = (og_ref[:, at].astype(F32) + part).astype(BF16)
+        part = dot(lg, near_ref[TOK:, at], 0, 0)
+        out_ref[:, at] = (near_ref[:TOK, at].astype(F32) + part).astype(BF16)
         copies.append(pltpu.make_async_copy(out_ref.at[:, at], out_hbm.at[:, at], sems.at[i]))
         copies[i].start()
     for copy in copies:
@@ -259,13 +268,14 @@
 def pack(og, li, rw, ids):
     return call(
         pack_kernel,
-        struct((PEERS, CHUNK, WIDE), BF16),
+        (struct((PEERS, CHUNK, WIDE), BF16), struct((TOK + PEERS, PARTS * WIDE), BF16)),
         [pltpu.VMEM(a.shape, a.dtype) for a in (og, li, rw, ids)]
         + [pltpu.VMEM((PEERS, WIDE), F32)] * 2
-        + [pltpu.SemaphoreType.DMA((4,))],
+        + [pltpu.SemaphoreType.DMA((6,))],
         flops=10**9,
         moved=2 * 10**6,
         in_specs=[far()] * 4,
+        out_specs=(whole(), far()),
         name="pack",
     )(og, li, rw, ids)
 
@@ -308,16 +318,17 @@
     )(me, s, code, gate)
 
 
-def input_grads(lg, og, rw):
+def input_grads(lg, near):
+    shape = (TOK, PARTS * WIDE)
     return call(
         input_kernel,
-        struct(og.shape, BF16),
-        [pltpu.VMEM(og.shape, BF16), pltpu.SemaphoreType.DMA((2,))],
+        struct(shape, BF16),
+        [pltpu.VMEM(shape, BF16), pltpu.SemaphoreType.DMA((2,))],
         flops=10**7,
         moved=10**6,
         out_specs=far(),
         name="inputs",
-    )(lg, og, rw)
+    )(lg, near)
 
 
 def router_grads(s, code, gate, recv, tie):
@@ -329,7 +340,7 @@
             pltpu.VMEM((128, CAP * 128), BF16),
             pltpu.VMEM((PEERS, PEERS * TOK), BF16),
         ],
-        flops=10**9,
+        flops=40 * 10**8,
         moved=2 * 10**6,
         name="router",
     )(s, code, gate, recv, tie)
@@ -350,19 +361,18 @@
     ids = jnp.swapaxes(expert_ids[0], 0, 1)
     far_args = [pltpu.with_memory_space_constraint(a, pltpu.HBM) for a in (og, li, rw, ids)]
     me = lax.axis_index("expert").astype(jnp.int32).reshape(1)
-    send = pack(*far_args)
+    send, near = pack(*far_args)
     recv = exchange(send)
     hidden_near, sdg = expert(
         recv, down_weight[0, 0], hidden_act[0, 0], jnp.asarray(compaction(), BF16)
     )
     back = exchange(sdg.reshape(PEERS, 1, SLOTS)).reshape(PEERS * 3, 128)
-    og_held, rw_held, sdg = lax.optimization_barrier((og, rw, sdg))
-    og_next, rw_next = shifted(og_held), shifted(rw_held)
+    near_next = shifted(near)
     all_gate, all_code, hidden_grad = side(recv, hidden_near)
     logit_grad = logit_grads(me, back, all_code, all_gate)
     logit_next = shifted(logit_grad)
     router_grad = router_grads(back, all_code, all_gate, recv, logit_grad)
-    sent = input_grads(logit_next, og_next, rw_next)[None]
+    sent = input_grads(logit_next, near_next)[None]
     return sent, hidden_grad[None, None], router_grad[None]
 
 

time: 99.7 us -> 99.7 us (level)
    ppermute x3 -> x2, starting transfers between devices: 21.2 us -> 21.2 us  [shifted(): return lax.ppermute(x, 'section', [(i, (i - 1) % n) for i in range(n)])]
  transfers between devices with their start and end apart: 4 -> 3, of which waited for: 0 -> 0; matrix products, arithmetic and copies ran while one was open for 0% -> 0% of each run, Pallas kernels for 3% -> 3%
where the time goes in v7:
time: 99.7 us; the launch traced here: 99.4 us
  blocking collectives  63.1 us (63%)
  starting transfers between devices  27.3 us (27%)
  Pallas kernels  8.23 us (8%)
    all_to_all x1, blocking collectives, exchange(): return lax.all_to_all(x, 'expert', split_axis=0, concat_axis=0, tiled=True)  63.1 us
    ppermute x2, starting transfers between devices, shifted(): return lax.ppermute(x, 'section', [(i, (i - 1) % n) for i in range(n)])  21.2 us
    all_to_all x1, starting transfers between devices, exchange(): return lax.all_to_all(x, 'expert', split_axis=0, concat_axis=0, tiled=True)  6.09 us
    pallas_call x1, Pallas kernels, pack(): call(pack_kernel, (struct((PEERS, CHUNK, WIDE), BF16), struct((TOK + PEER...  2.43 us
    pallas_call x1, Pallas kernels, expert(): call(expert_kernel, (struct((SLOTS, SLOTS), BF16), struct((PEERS * 3, 128...  2.12 us
  transfers between devices with their start and end apart: 3, of which 0 were waited for; matrix products, arithmetic and copies ran while one was open for 0% of the time, Pallas kernels for 3%

profile of v7, /device:TPU:1, one launch (start us, length us, event | category | flops | bytes accessed | tf_op | source)
XLA Modules:
  0.0 99.4 jit_solution(15372639653016980629)
XLA Ops:
  0.6 2.4 %pack.1 = (bf16[64,56,256]{2,1,0:T(8,128)(2,1)S(1)}, bf16[96,2048]{1,0:T(8,128)(2,1)S(1)}) custom-call(bf16[32,2048]{1,0:T(8,128)(2,1)} %bitcast.23, bf16[32,2048]{1,0:T(8,128)(2,1)} %bitcast.24, bf16[64,2048]{1,0:T(8,128)(2,1)} %bitcast.22, s32[8,32]{1,0:T(8,128)} %bitcast.25), custom_call_target="tpu_custom_call" | custom-call | flops 1000000000 | bytes 2000000 | tf_op jit(solution)/shard_map/pack/pallas_call | solution.py:269
  3.1 0.0 copy-start
  3.1 0.0 copy-start.1
  3.1 0.0 copy-start.2
  3.1 63.1 %all_to_all.10.recv_ref = bf16[64,56,256]{2,1,0:T(8,128)(2,1)S(1)} all-to-all(bf16[64,56,256]{2,1,0:T(8,128)(2,1)S(1)} %get-tuple-element.10), channel_id=1, replica_groups=mesh['section'=16,'expert'=64] {'expert'}, dimensions={0} | all-to-all | bytes 3670016 | tf_op jit(solution)/shard_map/all_to_all | solution.py:355
  66.2 0.0 copy-done
  66.2 0.0 copy-done.1
  66.2 0.0 copy-done.2
  66.2 2.1 %expert.1 = (bf16[384,384]{1,0:T(8,128)(2,1)S(1)}, f32[192,128]{1,0:T(8,128)}) custom-call(bf16[64,56,256]{2,1,0:T(8,128)(2,1)S(1)} %all_to_all.10.recv_ref, bf16[384,2048]{1,0:T(8,128)(2,1)S(1)} %bitcast.18, bf16[384,384]{1,0:T(8,128)(2,1)S(1)} %bitcast.19, bf16[192,192]{1,0:T(8,128)(2,1)S(1)} %copy-done.2), custom_call_target="tpu_custom_call" | custom-call | flops 1200000000 | bytes 4000000 | tf_op jit(solution)/shard_map/expert/pallas_call | solution.py:284
  68.3 6.1 %all-to-all-start.1 = ((f32[64,1,384]{2,1,0:T(1,128)}), f32[64,1,384]{2,1,0:T(1,128)S(1)}, u32[]{:S(2)}, u32[]{:S(2)}) async-start(f32[64,1,384]{2,1,0:T(1,128)} %bitcast.9), calls=%async_computation.1 | async-start | bytes 196608 | tf_op jit(solution)/shard_map/all_to_all | solution.py:355
  74.4 11.8 %collective-permute-start.1 = (bf16[96,2048]{1,0:T(8,128)(2,1)S(1)}, bf16[96,2048]{1,0:T(8,128)(2,1)S(1)}, u32[]{:S(2)}, u32[]{:S(2)}) collective-permute-start(bf16[96,2048]{1,0:T(8,128)(2,1)S(1)} %get-tuple-element.15), channel_id=1, source_target_pairs={{0,960},{64,0},{128,64},{192,128},{256,192},{320,256},{384,320},{4... | collective-permute-start | bytes 1179656 | tf_op jit(solution)/shard_map/ppermute | solution.py:351
  86.2 0.7 side.1
  87.0 0.0 all-to-all-done.1
  87.0 0.2 logits.1.tie_ref
  87.2 9.4 %collective-permute-start = (bf16[64,32]{1,0:T(8,128)(2,1)S(1)}, bf16[64,32]{1,0:T(8,128)(2,1)S(1)}, u32[]{:S(2)}, u32[]{:S(2)}) collective-permute-start(bf16[64,32]{1,0:T(8,128)(2,1)S(1)} %logits.1.tie_ref), channel_id=1, source_target_pairs={{0,960},{64,0},{128,64},{192,128},{256,192},{320,256},{384,320},{4... | collective-permute-start | bytes 12296 | tf_op jit(solution)/shard_map/ppermute | solution.py:351
  96.7 1.8 %router.1 = f32[32,64]{1,0:T(8,128)} custom-call(f32[192,128]{1,0:T(8,128)S(1)} %bitcast.17, bf16[16,64,128]{2,1,0:T(8,128)(2,1)S(1)} %get-tuple-element.13.code_ref, bf16[16,64,128]{2,1,0:T(8,128)(2,1)S(1)} %get-tuple-element.14.gate_ref, bf16[64,56,256]{2,1,0:T(8,128)(2,1)S(1)} %all_to_all.10.recv_ref, bf16[64,32]{1,0:T(8,128)(2,1)S(1)} %logits.1.tie_ref), custom_call_target="tpu_custom_call" | custom-call | flops 4000000000 | bytes 2000000 | tf_op jit(solution)/shard_map/router/pallas_call | solution.py:335
  98.5 0.0 collective-permute-done.1.near_ref
  98.5 0.0 collective-permute-done.lg_ref
  98.5 0.9 inputs.1
Async XLA Ops:
  3.1 63.1 %copy-start = (bf16[1,1,384,2048]{3,2,1,0:T(8,128)(2,1)S(1)}, bf16[1,1,384,2048]{3,2,1,0:T(8,128)(2,1)}, u32[]{:S(2)}) copy-start(bf16[1,1,384,2048]{3,2,1,0:T(8,128)(2,1)} %param.12) | copy-start | bytes 4718596
  3.1 63.1 %copy-start.1 = (bf16[1,1,384,384]{3,2,1,0:T(8,128)(2,1)S(1)}, bf16[1,1,384,384]{3,2,1,0:T(8,128)(2,1)}, u32[]{:S(2)}) copy-start(bf16[1,1,384,384]{3,2,1,0:T(8,128)(2,1)} %param.11) | copy-start | bytes 884740
  3.1 63.1 %copy-start.2 = (bf16[192,192]{1,0:T(8,128)(2,1)S(1)}, bf16[192,192]{1,0:T(8,128)(2,1)}, u32[]{:S(2)}) copy-start(bf16[192,192]{1,0:T(8,128)(2,1)} %constant.6.clone.perm_ref) | copy-start | bytes 221188
  68.3 18.7 %all-to-all-start.1 = ((f32[64,1,384]{2,1,0:T(1,128)}), f32[64,1,384]{2,1,0:T(1,128)S(1)}, u32[]{:S(2)}, u32[]{:S(2)}) async-start(f32[64,1,384]{2,1,0:T(1,128)} %bitcast.9), calls=%async_computation.1 | async-start | bytes 196608 | tf_op jit(solution)/shard_map/all_to_all | solution.py:355
  74.4 24.1 %collective-permute-start.1 = (bf16[96,2048]{1,0:T(8,128)(2,1)S(1)}, bf16[96,2048]{1,0:T(8,128)(2,1)S(1)}, u32[]{:S(2)}, u32[]{:S(2)}) collective-permute-start(bf16[96,2048]{1,0:T(8,128)(2,1)S(1)} %get-tuple-element.15), channel_id=1, source_target_pairs={{0,960},{64,0},{128,64},{192,128},{256,192},{320,256},{384,320},{4... | collective-permute-start | bytes 1179656 | tf_op jit(solution)/shard_map/ppermute | solution.py:351
  87.2 11.3 %collective-permute-start = (bf16[64,32]{1,0:T(8,128)(2,1)S(1)}, bf16[64,32]{1,0:T(8,128)(2,1)S(1)}, u32[]{:S(2)}, u32[]{:S(2)}) collective-permute-start(bf16[64,32]{1,0:T(8,128)(2,1)S(1)} %logits.1.tie_ref), channel_id=1, source_target_pairs={{0,960},{64,0},{128,64},{192,128},{256,192},{320,256},{384,320},{4... | collective-permute-start | bytes 12296 | tf_op jit(solution)/shard_map/ppermute | solution.py:351
